TPU v7x, 256 devices: a whole 4x4x8 slice. The times are simulated.
256 devices in a mesh: space: 32 (over y, z_lo, core), event: 8 (over x, z_hi).
Axes of the slice: x: 4, y: 4, z: 8 (z_hi: 2, z_lo: 4; z = z_hi * 4 + z_lo), core: 2. Of those that a mesh axis runs over, the one named last changes fastest.
Arguments:
- fwd_now: float32 [16, 64, 32768], P('event', None, 'space'), as said below
- fwd_prev: float32 [16, 64, 32768], P('event', None, 'space'), as said below
- adj_now: float32 [16, 64, 32768], P('event', None, 'space'), as said below
- adj_prev: float32 [16, 64, 32768], P('event', None, 'space'), as said below
- shear_mod: float32 [64, 32768], P(None, 'space'), may hold values from 0.5 to 2
- density: float32 [32768], P('space'), may hold values from 0.5 to 2
- station_owner: int32 [65536, 1], P('space'), may hold values from 0 to 31; in each aligned block of 2048 rows (0 to 2047, 2048 to 4095, ...) at most 256 rows name the same one
- receiver_local: int32 [65536], P('space'), may hold values from 0 to 1023
- station_weights: float32 [64, 65536], P(None, 'space'), may hold values from -6 to 6
- adj_records: float32 [16, 2, 65536], P('event', None, 'space'), may hold values from -6 to 6
Outputs:
- fwd_last: float32 [16, 64, 32768], P('event', None, 'space')
- fwd_before: float32 [16, 64, 32768], P('event', None, 'space')
- adj_last: float32 [16, 64, 32768], P('event', None, 'space')
- adj_before: float32 [16, 64, 32768], P('event', None, 'space')
- kernel: float32 [64, 32768], P(None, ('space', 'event'))
Inputs may be any that keep to these rules, and one draw needn't show every extreme that they name: `station_owner`: the 2048 stations of one index of space name at most 256 with the same owner. `fwd_now`: each displacement is continuous: element-local copies of a shared node hold equal values. `fwd_prev`: continuous like fwd_now. `adj_now`: continuous like fwd_now. `adj_prev`: continuous like fwd_now.
All inputs are finite; a program needn't handle non-finite values.
Results may differ from a plain program's by a relative error of at most 0.0001.
Values sent between devices are 32-bit elements; how exact they have to be, the bound alone decides.
A program may use at most 64 MiB of HBM per device.

v0:
```python
import jax
import jax.numpy as jnp
import numpy as np
from jax import lax
from jax.experimental import pallas as pl
from jax.experimental.pallas import tpu as pltpu
from jax.sharding import PartitionSpec as P

MESH = pl.DeviceIdType.MESH
DMA = pltpu.SemaphoreType.DMA
VM = pl.BlockSpec(memory_space=pltpu.VMEM)
F32 = jnp.float32
SLABS, EVENT, CAP, ST, ELEMS = 32, 8, 256, 2048, 1024
DIRECT = 32
TIME_STEP, STEP_SQUARE = 0.08, 0.0064


def derivative_table():
    root = 1.0 / np.sqrt(5.0)
    p = np.array([-1.0, -root, root, 1.0])
    d = np.zeros((4, 4))
    for i in range(4):
        for j in range(4):
            if i == j:
                d[i, i] = sum(1.0 / (p[i] - p[k]) for k in range(4) if k != i)
            else:
                upper = np.prod([p[i] - p[k] for k in range(4) if k not in (i, j)])
                lower = np.prod([p[j] - p[k] for k in range(4) if k != j])
                d[i, j] = upper / lower
    return d


D = derivative_table()
ALPHA, BETA = float((D[0, 0] + D[0, 3]) / 2), float((D[1, 0] + D[1, 3]) / 2)
B00, B01 = float((D[0, 0] - D[0, 3]) / 2), float((D[0, 1] - D[0, 2]) / 2)
B10, B11 = float((D[1, 0] - D[1, 3]) / 2), float((D[1, 1] - D[1, 2]) / 2)


def gradient(f):
    e, o0, o1 = (f[0] + f[3]) - (f[1] + f[2]), f[0] - f[3], f[1] - f[2]
    a0, a1 = ALPHA * e, BETA * e
    b0, b1 = B00 * o0 + B01 * o1, B10 * o0 + B11 * o1
    return [b0 + a0, b1 + a1, b1 - a1, b0 - a0]


def divergence(t):
    e0, e1, o0, o1 = t[0] + t[3], t[1] + t[2], t[0] - t[3], t[1] - t[2]
    r = ALPHA * o0 + BETA * o1
    q0, q1 = B00 * e0 + B10 * e1, B01 * e0 + B11 * e1
    return [r + q0, q1 - r, -q1 - r, r - q0]


def node_weight(n):
    def w(i):
        return jnp.where((i == 0) | (i == 3), np.float32(1.0 / 6.0), np.float32(5.0 / 6.0))

    return w(n % 4) * w(n // 4 % 4) * w(n // 16)


def coords():
    me, ev = lax.axis_index("space"), lax.axis_index("event")
    return me, ev, me // 8, me // 2 % 4, me % 2, ev // 2, ev % 2


def copy_to(src, dst, send, recv, **where):
    return pltpu.make_async_remote_copy(
        src_ref=src, dst_ref=dst, send_sem=send, recv_sem=recv, device_id=where, device_id_type=MESH
    )


def signal(barrier, inc=1, **where):
    pl.semaphore_signal(barrier, inc=inc, device_id=where, device_id_type=MESH)


def place_kernel(owner, ids, weights, records, send_w, send_r, tail, rows, placed, spots_v, spots, sem):
    x = lax.axis_index("event") // 2
    slab = lax.broadcasted_iota(jnp.int32, (SLABS, 256), 0)
    earlier = (
        lax.broadcasted_iota(jnp.int32, (256, 256), 0) < lax.broadcasted_iota(jnp.int32, (256, 256), 1)
    ).astype(F32).astype(jnp.bfloat16)
    named = [jnp.where(owner[b : b + 1, :] == slab, 1.0, 0.0).astype(F32) for b in range(8)]
    counts = jnp.dot(
        jnp.concatenate(named, axis=0).astype(jnp.bfloat16), earlier, preferred_element_type=F32
    )
    carry = jnp.zeros((SLABS, 1), F32)
    for b in range(8):
        rank = jnp.sum(named[b] * (counts[32 * b : 32 * b + 32] + carry), axis=0, keepdims=True)
        carry = carry + jnp.sum(named[b], axis=1, keepdims=True)
        spots_v[b : b + 1, :] = owner[b : b + 1, :] * CAP + rank.astype(jnp.int32)
    copy = pltpu.make_async_copy(spots_v, spots, sem)
    copy.start()
    tail[...] = jnp.zeros_like(tail)
    for k in range(4):
        tail[k : k + 1, :] = records[k // 2, k % 2 : k % 2 + 1, :]
    tail[4:5, :] = ids[...].astype(F32)
    for c in range(ST // 128):
        cols = slice(128 * c, 128 * c + 128)
        block = jnp.concatenate(
            [weights[pl.ds(pl.multiple_of((x + q) % 4 * 16, 16), 16), cols] for q in range(DIRECT // 16)]
            + [tail[:, cols], jnp.zeros((120 - DIRECT, 128), F32)],
            axis=0,
        )
        rows[cols, :] = block.T

    def clear(i, carry):
        placed[pl.ds(pl.multiple_of(i * 128, 128), 128), :] = jnp.zeros((128, 128), F32)
        return carry

    lax.fori_loop(0, SLABS * CAP // 128, clear, 0)
    copy.wait()

    def move(i, carry):
        for j in range(16):
            spot = spots[i // 16, i % 16 * 16 + j]
            placed[pl.ds(spot, 1), :] = rows[pl.ds(i * 16 + j, 1), :]
        return carry

    lax.fori_loop(0, ST // 16, move, 0)

    def turn(t, carry):
        for h in range(2):
            block = placed[pl.ds(pl.multiple_of(t * CAP + h * 128, 128), 128), :].T
            send_w[t, :, 128 * h : 128 * h + 128] = block[:DIRECT]
            for r in range(5):
                send_r[t, :, 256 * r + 128 * h : 256 * r + 128 * h + 128] = block[DIRECT + r : DIRECT + r + 1]
        return carry

    lax.fori_loop(0, SLABS, turn, 0)


def place(owner, ids, weights, records):
    return pl.pallas_call(
        place_kernel,
        out_shape=(
            jax.ShapeDtypeStruct((SLABS, DIRECT, CAP), F32),
            jax.ShapeDtypeStruct((SLABS, 1, 5 * CAP), F32),
        ),
        in_specs=[VM] * 4,
        out_specs=(VM, VM),
        scratch_shapes=[
            pltpu.VMEM((8, ST), F32),
            pltpu.VMEM((ST, 128), F32),
            pltpu.VMEM((SLABS * CAP, 128), F32),
            pltpu.VMEM((8, 256), jnp.int32),
            pltpu.SMEM((8, 256), jnp.int32),
            DMA,
        ],
        compiler_params=pltpu.CompilerParams(vmem_limit_bytes=40 << 20),
        name="place",
    )(owner, ids, weights, records)


def weight_goal(dy, dz):
    me, ev, y, z, c, x, half = coords()
    deep = half * 4 + z
    step = (0, 1, 7)[dz] if dz < 3 else 2 + 4 * ((deep // 2 + dy) % 2)
    deep = (deep + step) % 8
    return (y + dy) % 4 * 8 + deep % 4 * 2, x * 2 + deep // 4


def record_goal(dy, dz):
    me, ev, y, z, c, x, half = coords()
    return (y + dy) % 4 * 8 + (z + (0, 1, 3, 2)[dz]) % 4 * 2


def greet_stations(barrier):
    me, ev, y, z, c, x, half = coords()
    for dy in range(4):
        for dz in range(4):
            if dy == 0 and dz == 0:
                signal(barrier, 2, space=me + 1 - 2 * c)
                continue
            goal, event = weight_goal(dy, dz)
            other = record_goal(dy, dz)
            for c2 in range(2):
                signal(barrier, space=goal + c2, event=event)
                signal(barrier, space=other + c2)
    signal(barrier, event=(ev + 2) % 8)
    signal(barrier, event=(ev + 6) % 8)
    return 64


def send_stations(send_w, send_r, got_w, got_r, sw, rw, sr, rr):
    me, ev, y, z, c, x, half = coords()
    here = (0, 0, c)
    own = [
        pltpu.make_async_copy(send_w.at[me], got_w.at[here], rw.at[here]),
        pltpu.make_async_copy(send_r.at[me], got_r.at[here], rr.at[here]),
    ]
    for copy in own:
        copy.start()
    copies = []
    for dy in range(4):
        for dz in range(4):
            for c2 in range(2):
                if dy == 0 and dz == 0:
                    if c2 == 0:
                        continue
                    goal = other = me + 1 - 2 * c
                    event = ev
                else:
                    goal, event = weight_goal(dy, dz)
                    goal, other = goal + c2, record_goal(dy, dz) + c2
                mine, there = (dy, dz, c2), (dy, dz, c)
                copies += [
                    copy_to(send_w.at[goal], got_w.at[there], sw.at[mine], rw.at[there], space=goal, event=event),
                    copy_to(send_r.at[other], got_r.at[there], sr.at[mine], rr.at[there], space=other),
                ]
                copies[-2].start()
                copies[-1].start()
    return copies


def gather_sources(got_w, got_r, left, right, left_part, onehot, total, rw, rr, fs, fr):
    me, ev, y, z, c, x, half = coords()

    def shares(w):
        return (
            copy_to(got_w.at[w, :, :, 0:16], left.at[w], fs.at[w, 0], fr.at[w, 0], event=(ev + 2) % 8),
            copy_to(got_w.at[w, :, :, 16:32], right.at[w], fs.at[w, 1], fr.at[w, 1], event=(ev + 6) % 8),
        )

    def receive(w):
        for dz in range(4):
            for cs in range(2):
                at = (w, dz, cs)
                pltpu.make_async_copy(got_w.at[at], got_w.at[at], rw.at[at]).wait()
                pltpu.make_async_copy(got_r.at[at], got_r.at[at], rr.at[at]).wait()
        for copy in shares(w):
            copy.start()

    def add(w, carry):
        @pl.when(w < 3)
        def _():
            receive(w + 1)

        for copy in shares(w):
            copy.wait_recv()

        def block(k, carry):
            at = (w, k // 2, k % 2)
            cols = pl.ds(pl.multiple_of(k * CAP, CAP), CAP)
            nodes = jnp.concatenate([got_w[at], right[at], left[at]], axis=0)
            samples = got_r[at]
            for q in range(4):
                product = nodes * samples[:, 256 * q : 256 * q + 256]
                upper = product.astype(jnp.bfloat16)
                left_part[64 * q : 64 * q + 64, cols] = upper
                left_part[256 + 64 * q : 320 + 64 * q, cols] = (product - upper.astype(F32)).astype(jnp.bfloat16)
            spot = samples[:, 1024:1280].astype(jnp.int32)
            for i in range(8):
                row = lax.broadcasted_iota(jnp.int32, (128, CAP), 0) + 128 * i
                onehot[128 * i : 128 * i + 128, cols] = jnp.where(row == spot, 1.0, 0.0).astype(jnp.bfloat16)
            return carry

        lax.fori_loop(0, 8, block, 0)

        def columns(j, carry):
            at = pl.ds(pl.multiple_of(j * 256, 256), 256)
            total[j] = total[j] + lax.dot_general(
                left_part[...], onehot[at, :], (((1,), (1,)), ((), ())), preferred_element_type=F32
            )
            return carry

        lax.fori_loop(0, 4, columns, 0)
        return carry

    total[...] = jnp.zeros_like(total)
    receive(0)
    lax.fori_loop(0, 4, add, 0)


def spread_sources(total, src):
    x = lax.axis_index("event") // 2

    def tile(i, carry):
        q, r = i // 8, i % 8
        goal = q * 8 + (r // 2 + x) % 4 * 2 + r % 2
        for j in range(8):
            cols = slice(j % 2 * 128, j % 2 * 128 + 128)
            upper = total[j // 2, pl.ds(pl.multiple_of(i * 8, 8), 8), cols]
            lower = total[j // 2, pl.ds(pl.multiple_of(256 + i * 8, 8), 8), cols]
            src[pl.ds(pl.multiple_of(goal * 64 + j * 8, 8), 8), :] = upper + lower
        return carry

    lax.fori_loop(0, 32, tile, 0)


def row_of(n):
    return n // 8 * 64 + n % 8


def strided(base):
    return pl.ds(base, 8, stride=8)


def tile_of(n):
    return pl.ds(pl.multiple_of(n * 8, 8), 8)


def element_masks():
    sub = lax.broadcasted_iota(jnp.int32, (8, 128), 0)
    lane = lax.broadcasted_iota(jnp.int32, (8, 128), 1)
    return sub, lane


def from_before_x(v):
    sub, lane = element_masks()
    return jnp.where(lane % 16 != 0, pltpu.roll(v, 1, 1), 0.0)


def from_before_y(v):
    sub, lane = element_masks()
    turned = pltpu.roll(v, 16, 1)
    moved = jnp.where(lane < 16, pltpu.roll(turned, 1, 0), turned)
    return jnp.where((sub % 2 != 0) | (lane >= 16), moved, 0.0)


def after_x(v, old):
    sub, lane = element_masks()
    return jnp.where(lane % 16 != 15, pltpu.roll(v, 127, 1), old)


def after_y(v, old):
    sub, lane = element_masks()
    turned = pltpu.roll(v, 112, 1)
    moved = jnp.where(lane >= 112, pltpu.roll(turned, 7, 0), turned)
    return jnp.where((sub % 2 != 1) | (lane < 112), moved, old)


def stiffness(now, local, stiff, terms, first):
    def line(nodes, fresh, fresh_terms):
        mu = [stiff[n] for n in nodes]
        sums = [None] * 4
        for e in range(2):
            g = []
            for f in (e, e + 2):
                grad = gradient([now[f * 64 + n] for n in nodes])
                out = divergence([a * b for a, b in zip(grad, mu)])
                for n, value in zip(nodes, out):
                    local[f * 64 + n] = value if fresh else local[f * 64 + n] + value
                g.append(grad)
            for i in range(4):
                pair = g[0][i] * g[1][i]
                sums[i] = pair if e == 0 else sums[i] + pair
        for n, value in zip(nodes, sums):
            terms[tile_of(n), :] = value if fresh_terms else terms[tile_of(n), :] + value

    def along_a(l, carry):
        line([4 * l + i for i in range(4)], True, first)
        return carry

    def along_b(l, carry):
        line([l // 4 * 16 + l % 4 + 4 * i for i in range(4)], False, False)
        return carry

    def along_c(l, carry):
        line([l + 16 * i for i in range(4)], False, False)
        return carry

    for body in (along_a, along_b, along_c):
        lax.fori_loop(0, 16, body, 0)


def assemble_xy(local, first, count):
    def along_x(l, carry):
        at = first * 64 + 4 * l
        low, high = local[at], local[at + 3]
        new = low + from_before_x(high)
        local[at] = new
        local[at + 3] = after_x(new, high)
        return carry

    def along_y(l, carry):
        at = first * 64 + l // 4 * 16 + l % 4
        low, high = local[at], local[at + 12]
        new = low + from_before_y(high)
        local[at] = new
        local[at + 12] = after_y(new, high)
        return carry

    lax.fori_loop(0, 16 * count, along_x, 0)
    lax.fori_loop(0, 16 * count, along_y, 0)


def pack_faces(local, faces):
    sub, lane = element_masks()

    def group(i, carry):
        base = i // 4 * 64 + i % 4 * 4
        low = local[base]
        high = pltpu.roll(local[base + 48], 2, 0)
        for q in range(1, 4):
            low = jnp.where(sub // 2 == q, pltpu.roll(local[base + q], 2 * q, 0), low)
            high = jnp.where(sub // 2 == q, pltpu.roll(local[base + 48 + q], (2 * q + 2) % 8, 0), high)
        faces[0, i] = low
        faces[1, i] = high
        return carry

    lax.fori_loop(0, 16, group, 0)


def assemble_z(local, got):
    me = lax.axis_index("space")
    sub, lane = element_masks()

    def group(i, carry):
        base = i // 4 * 64 + i % 4 * 4
        before = jnp.where(me > 0, got[0, i], 0.0)
        after = jnp.where(me < SLABS - 1, got[1, i], 0.0)
        for q in range(4):
            low, high = local[base + q], local[base + 48 + q]
            mine = pltpu.roll(before, (8 - 2 * q) % 8, 0) if q else before
            new = low + jnp.where(sub < 2, mine, pltpu.roll(high, 2, 0))
            theirs = pltpu.roll(after, (6 - 2 * q) % 8, 0) if q < 3 else after
            local[base + q] = new
            local[base + 48 + q] = jnp.where(sub < 6, pltpu.roll(new, 6, 0), high + theirs)
        return carry

    lax.fori_loop(0, 16, group, 0)


def inverse_mass(density, got, table, inv):
    me = lax.axis_index("space")
    sub, lane = element_masks()

    def planes(v):
        out = []
        low = v + from_before_x(v)
        for a in (low, v, after_x(low, v)):
            new = a + from_before_y(a)
            out += [(new, a, after_y(new, a))]
        return out

    here = planes(density)
    before = planes(jnp.where(me > 0, got[0], 0.0))
    after = planes(jnp.where(me < SLABS - 1, got[1], 0.0))
    for a in range(3):
        for b in range(3):
            v = here[a][b]
            low = v + jnp.where(sub < 2, pltpu.roll(before[a][b], 2, 0), pltpu.roll(v, 2, 0))
            high = v + jnp.where(sub < 6, pltpu.roll(v, 6, 0), pltpu.roll(after[a][b], 6, 0))
            for c, value in enumerate((low, v, high)):
                table[9 * c + 3 * b + a] = 1.0 / value

    def node(n, carry):
        def part(i):
            return (i + 1) // 2

        at = part(n // 16) * 9 + part(n // 4 % 4) * 3 + part(n % 4)
        inv[n] = table[at] * (np.float32(STEP_SQUARE) / node_weight(n))
        return carry

    lax.fori_loop(0, 64, node, 0)


def step_kernel(
    send_w, send_r, fwd_now, fwd_prev, adj_now, adj_prev, shear, density,
    one, two, pieces,
    got_w, got_r, left, right, left_part, onehot, total, src,
    zero, local, stiff, inv, table, terms, faces, got_faces, got_density, out_terms,
    sw, rw, sr, rr, fs, fr, hs, hr, ds, dr, ts, tr,
):
    me, ev, y, z, c, x, half = coords()
    up, down = (me + 1) % SLABS, (me + SLABS - 1) % SLABS
    barrier = pltpu.get_barrier_semaphore()
    greeted = greet_stations(barrier)
    for k in range(1, EVENT):
        signal(barrier, event=(ev + k) % EVENT)
    signal(barrier, space=up)
    signal(barrier, space=down)

    def load(n, carry):
        for f, ref in enumerate((fwd_now, adj_now)):
            for e in range(2):
                zero[(2 * f + e) * 64 + n] = ref[strided(e * 512 + row_of(n)), :]
        stiff[n] = shear[strided(row_of(n)), :] * node_weight(n)
        return carry

    lax.fori_loop(0, 64, load, 0)
    pl.semaphore_wait(barrier, greeted + EVENT - 1 + 2)

    copies = send_stations(send_w, send_r, got_w, got_r, sw, rw, sr, rr)
    weigh = [
        copy_to(density, got_density.at[1], ds.at[1], dr.at[1], space=down),
        copy_to(density, got_density.at[0], ds.at[0], dr.at[0], space=up),
    ]
    for copy in weigh:
        copy.start()

    stiffness(zero, local, stiff, terms, True)
    assemble_xy(local, 0, 2)
    for copy in weigh:
        copy.wait()
    inverse_mass(density[...], got_density, table, inv)

    gather_sources(got_w, got_r, left, right, left_part, onehot, total, rw, rr, fs, fr)
    spread_sources(total, src)

    now, later = zero, one
    for step in range(2):
        def less(n, carry):
            for e in range(2):
                at = (2 + e) * 64 + n
                local[at] = local[at] - src[strided((2 * e + step) * 512 + row_of(n)), :]
            return carry

        lax.fori_loop(0, 64, less, 0)
        if step == 0:
            assemble_xy(local, 2, 2)
        else:
            assemble_xy(local, 0, 4)
        pack_faces(local, faces.at[step])
        halo = [
            copy_to(faces.at[step, 0], got_faces.at[step, 1], hs.at[step, 0], hr.at[step, 0], space=down),
            copy_to(faces.at[step, 1], got_faces.at[step, 0], hs.at[step, 1], hr.at[step, 1], space=up),
        ]
        for copy in halo:
            copy.start()
        copies += halo
        for copy in halo:
            copy.wait_recv()
        assemble_z(local, got_faces.at[step])

        def update(n, carry):
            mine = inv[n]
            for f in range(4):
                at = f * 64 + n
                if step == 0:
                    old = (fwd_prev, adj_prev)[f // 2][strided(f % 2 * 512 + row_of(n)), :]
                else:
                    old = zero[at]
                later[at] = 2.0 * now[at] - old - local[at] * mine
            return carry

        lax.fori_loop(0, 64, update, 0)
        if step == 0:
            stiffness(one, local, stiff, terms, False)
            now, later = one, two

            def cut(j, carry):
                out_terms[j] = terms[pl.ds(j, 64, stride=8), :]
                return carry

            lax.fori_loop(0, EVENT, cut, 0)
            for k in range(1, EVENT):
                goal = (ev + k) % EVENT
                copies.append(copy_to(out_terms.at[goal], pieces.at[k], ts.at[k], tr.at[k], event=goal))
                copies[-1].start()
            pieces[0] = out_terms[ev]

    for copy in copies[-9:-2]:
        copy.wait_recv()
    for copy in copies:
        copy.wait_send()

    def last(w, carry):
        copy_to(got_w.at[w, :, :, 0:16], left.at[w], fs.at[w, 0], fr.at[w, 0], event=(ev + 2) % 8).wait_send()
        copy_to(got_w.at[w, :, :, 16:32], right.at[w], fs.at[w, 1], fr.at[w, 1], event=(ev + 6) % 8).wait_send()
        return carry

    lax.fori_loop(0, 4, last, 0)


def steps(send_w, send_r, fwd_now, fwd_prev, adj_now, adj_prev, shear, density):
    fields = pltpu.VMEM((256, 8, 128), F32)
    waves = DMA((4, 4, 2))
    return pl.pallas_call(
        step_kernel,
        out_shape=(
            jax.ShapeDtypeStruct((256, 8, 128), F32),
            jax.ShapeDtypeStruct((256, 8, 128), F32),
            jax.ShapeDtypeStruct((EVENT, 64, 128), F32),
        ),
        in_specs=[VM] * 8,
        out_specs=(VM, VM, VM),
        scratch_shapes=[
            pltpu.VMEM((4, 4, 2, DIRECT, CAP), F32),
            pltpu.VMEM((4, 4, 2, 1, 5 * CAP), F32),
            pltpu.VMEM((4, 4, 2, 16, CAP), F32),
            pltpu.VMEM((4, 4, 2, 16, CAP), F32),
            pltpu.VMEM((512, 8 * CAP), jnp.bfloat16),
            pltpu.VMEM((ELEMS, 8 * CAP), jnp.bfloat16),
            pltpu.VMEM((4, 512, 256), F32),
            pltpu.VMEM((2048, 128), F32),
            fields,
            fields,
            pltpu.VMEM((64, 8, 128), F32),
            pltpu.VMEM((64, 8, 128), F32),
            pltpu.VMEM((27, 8, 128), F32),
            pltpu.VMEM((512, 128), F32),
            pltpu.VMEM((2, 2, 16, 8, 128), F32),
            pltpu.VMEM((2, 2, 16, 8, 128), F32),
            pltpu.VMEM((2, 8, 128), F32),
            pltpu.VMEM((EVENT, 64, 128), F32),
            waves, waves, waves, waves,
            DMA((4, 2)), DMA((4, 2)),
            DMA((2, 2)), DMA((2, 2)),
            DMA((2,)), DMA((2,)),
            DMA((EVENT,)), DMA((EVENT,)),
        ],
        compiler_params=pltpu.CompilerParams(collective_id=0, has_side_effects=True, vmem_limit_bytes=56 << 20),
        name="steps",
    )(send_w, send_r, fwd_now, fwd_prev, adj_now, adj_prev, shear, density)


def finish_kernel(one, two, pieces, shear, fwd_last, fwd_before, adj_last, adj_before, kernel):
    ev = lax.axis_index("event")

    def node(n, carry):
        for f in range(4):
            last, before = ((fwd_last, fwd_before), (adj_last, adj_before))[f // 2]
            at = strided(f % 2 * 512 + row_of(n))
            before[at, :] = one[f * 64 + n]
            last[at, :] = two[f * 64 + n]
        return carry

    lax.fori_loop(0, 64, node, 0)
    for b in range(8):
        rows = slice(8 * b, 8 * b + 8)
        total = pieces[0, rows]
        for k in range(1, EVENT):
            total = total + pieces[k, rows]
        n = 8 * b + lax.broadcasted_iota(jnp.int32, (8, 128), 0)
        factor = node_weight(n) * np.float32(-TIME_STEP)
        kernel[rows, :] = total * (factor * shear[pl.ds(pl.multiple_of(b * 64 + ev * 8, 8), 8), :])


def finish(one, two, pieces, shear):
    return pl.pallas_call(
        finish_kernel,
        out_shape=(*[jax.ShapeDtypeStruct((1024, 128), F32)] * 4, jax.ShapeDtypeStruct((64, 128), F32)),
        in_specs=[VM] * 4,
        out_specs=(VM,) * 5,
        compiler_params=pltpu.CompilerParams(vmem_limit_bytes=30 << 20),
        name="finish",
    )(one, two, pieces, shear)


def to_rows(field):
    count = field.size // (64 * ELEMS)
    return field.reshape(count, 8, 8, 8, 128).transpose(0, 1, 3, 2, 4).reshape(count * 512, 128)


def from_rows(rows):
    return rows.reshape(2, 8, 8, 8, 128).transpose(0, 1, 3, 2, 4).reshape(2, 64, ELEMS)


def shards(
    fwd_now, fwd_prev, adj_now, adj_prev, shear_mod, density, station_owner, receiver_local, station_weights, adj_records
):
    shear = to_rows(shear_mod)
    send_w, send_r = place(
        station_owner.reshape(8, 256), receiver_local.reshape(1, ST), station_weights, adj_records
    )
    one, two, pieces = steps(
        send_w, send_r, to_rows(fwd_now), to_rows(fwd_prev), to_rows(adj_now), to_rows(adj_prev),
        shear, density.reshape(8, 128),
    )
    *fields, kernel = finish(one, two, pieces, shear)
    return (*map(from_rows, fields), kernel)


def solution(mesh):
    fields = P("event", None, "space")
    return jax.shard_map(
        shards,
        mesh=mesh,
        in_specs=(
            fields, fields, fields, fields,
            P(None, "space"), P("space"), P("space", None), P("space"), P(None, "space"), fields,
        ),
        out_specs=(fields, fields, fields, fields, P(None, ("space", "event"))),
        check_vma=False,
    )
```

profile of v0, /device:TPU:2, one launch (start us, length us, event | category | flops | bytes accessed | tf_op | source)
XLA Modules:
  0.0 124.2 jit_solution(15636996941336756933)
XLA Ops:
  0.6 0.0 copy-start.7
  0.6 0.5 broadcast.3
  1.2 1.4 %reduce.3 = s32[2048]{0:T(1024)S(1)} reduce(s32[2048,1]{0,1:T(1,128)} %param.16, s32[]{:T(128)} %broadcast.3), dimensions={1}, to_apply=%param.16.reduce_sub_computation.3 | reduce | bytes 16388 | tf_op args[6]
  2.5 0.0 copy-start.8
  2.5 0.0 copy-done.7
  2.6 0.7 copy-done.8
  3.2 0.0 copy-start.4
  3.2 1.0 copy-done.4
  4.3 9.9 %place.1 = (f32[32,32,256]{2,1,0:T(8,128)S(1)}, f32[32,1,1280]{2,1,0:T(1,128)S(1)}) custom-call(s32[8,256]{1,0:T(8,128)S(1)} %reshape.73.owner, s32[1,2048]{1,0:T(1,128)S(1)} %bitcast.50, f32[64,2048]{1,0:T(8,128)S(1)} %copy-done.4, f32[2,2,2048]{2,1,0:T(2,128)S(1)} %copy-done.7), custom_call_target="tpu_custom_call" | custom-call | tf_op jit(solution)/shard_map/place/pallas_call | solution.py:132
  14.2 0.0 copy-start.2
  14.2 1.0 copy-done.2
  15.1 0.0 copy-start.6
  15.1 0.7 copy-done.6
  15.8 0.0 copy-start.3
  15.8 102.8 %steps.1 = (f32[256,8,128]{2,1,0:T(8,128)}, f32[256,8,128]{2,1,0:T(8,128)}, f32[8,64,128]{2,1,0:T(8,128)}) custom-call(f32[32,32,256]{2,1,0:T(8,128)} %copy-done.2, f32[32,1,1280]{2,1,0:T(1,128)} %copy-done.6, f32[1024,128]{1,0:T(8,128)} %bitcast.51, f32[1024,128]{1,0:T(8,128)} %bitcast.52, f32[1024,128]{1,0:T(8,128)} %bitcast.53, f32[1024,128]{1,0:T(8,128)} %bitcast.54, ...), custom_call_target="tpu_custom_call" | custom-call | tf_op jit(solution)/shard_map/steps/pallas_call | solution.py:568
  118.6 0.0 copy-done.3
  118.6 0.0 copy-start
  118.6 1.2 copy-done
  119.9 0.0 copy-start.1
  119.9 1.2 copy-done.1
  121.1 0.0 copy-start.5
  121.1 0.9 copy-done.5
  122.0 2.2 %finish.1 = (f32[1024,128]{1,0:T(8,128)}, f32[1024,128]{1,0:T(8,128)}, f32[1024,128]{1,0:T(8,128)}, f32[1024,128]{1,0:T(8,128)}, f32[64,128]{1,0:T(8,128)}) custom-call(f32[256,8,128]{2,1,0:T(8,128)S(1)} %copy-done, f32[256,8,128]{2,1,0:T(8,128)S(1)} %copy-done.1, f32[8,64,128]{2,1,0:T(8,128)S(1)} %copy-done.5, f32[512,128]{1,0:T(8,128)S(1)} %bitcast.49), custom_call_target="tpu_custom_call" | custom-call | tf_op jit(solution)/shard_map/finish/pallas_call | solution.py:630
  (1 shorter events, 0.0 us)
Async XLA Ops:
  0.6 1.9 %copy-start.7 = (f32[2,2,2048]{2,1,0:T(2,128)S(1)}, f32[2,2,2048]{2,1,0:T(2,128)}, u32[]{:S(2)}) copy-start(f32[2,2,2048]{2,1,0:T(2,128)} %records.1) | copy-start | bytes 98308
  2.5 0.7 copy-start.8
  3.2 1.0 copy-start.4
  14.2 1.0 copy-start.2
  15.1 0.7 copy-start.6
  15.8 102.8 %copy-start.3 = (f32[64,1024]{1,0:T(8,128)S(1)}, f32[64,1024]{1,0:T(8,128)}, u32[]{:S(2)}) copy-start(f32[64,1024]{1,0:T(8,128)} %param.14) | copy-start | bytes 786436
  118.6 1.2 copy-start
  119.9 1.2 copy-start.1
  121.1 0.9 copy-start.5
where the time goes:
time: 125 us; the launch traced here: 124 us
  Pallas kernels  115 us (92%)
  local copies, waits for them, and re-layouts  7.25 us (6%)
  other arithmetic  1.36 us (1%)
    pallas_call x1, Pallas kernels, steps(): pl.pallas_call(step_kernel, out_shape=(jax.ShapeDtypeStruct((256, 8, 128)...  103 us
    pallas_call x1, Pallas kernels, place(): pl.pallas_call(place_kernel, out_shape=(jax.ShapeDtypeStruct((SLABS, DIRE...  9.88 us
    unnamed x19, local copies, waits for them, and re-layouts  7.24 us

commit v1 on v0

v1 whole, which is shorter than its diff:
```python
import jax
import jax.numpy as jnp
import numpy as np
from jax import lax
from jax.experimental import pallas as pl
from jax.experimental.pallas import tpu as pltpu
from jax.sharding import PartitionSpec as P

MESH = pl.DeviceIdType.MESH
DMA = pltpu.SemaphoreType.DMA
VM = pl.BlockSpec(memory_space=pltpu.VMEM)
HBM = pl.BlockSpec(memory_space=pltpu.HBM)
F32 = jnp.float32
SLABS, EVENT, CAP, ST, ELEMS = 32, 8, 256, 2048, 1024
DIRECT = 32
TIME_STEP, STEP_SQUARE = 0.08, 0.0064


def derivative_table():
    root = 1.0 / np.sqrt(5.0)
    p = np.array([-1.0, -root, root, 1.0])
    d = np.zeros((4, 4))
    for i in range(4):
        for j in range(4):
            if i == j:
                d[i, i] = sum(1.0 / (p[i] - p[k]) for k in range(4) if k != i)
            else:
                upper = np.prod([p[i] - p[k] for k in range(4) if k not in (i, j)])
                lower = np.prod([p[j] - p[k] for k in range(4) if k != j])
                d[i, j] = upper / lower
    return d


D = derivative_table()
ALPHA, BETA = float((D[0, 0] + D[0, 3]) / 2), float((D[1, 0] + D[1, 3]) / 2)
B00, B01 = float((D[0, 0] - D[0, 3]) / 2), float((D[0, 1] - D[0, 2]) / 2)
B10, B11 = float((D[1, 0] - D[1, 3]) / 2), float((D[1, 1] - D[1, 2]) / 2)


def gradient(f):
    e, o0, o1 = (f[0] + f[3]) - (f[1] + f[2]), f[0] - f[3], f[1] - f[2]
    a0, a1 = ALPHA * e, BETA * e
    b0, b1 = B00 * o0 + B01 * o1, B10 * o0 + B11 * o1
    return [b0 + a0, b1 + a1, b1 - a1, b0 - a0]


def divergence(t):
    e0, e1, o0, o1 = t[0] + t[3], t[1] + t[2], t[0] - t[3], t[1] - t[2]
    r = ALPHA * o0 + BETA * o1
    q0, q1 = B00 * e0 + B10 * e1, B01 * e0 + B11 * e1
    return [r + q0, q1 - r, -q1 - r, r - q0]


def node_weight(n):
    def w(i):
        return jnp.where((i == 0) | (i == 3), np.float32(1.0 / 6.0), np.float32(5.0 / 6.0))

    return w(n % 4) * w(n // 4 % 4) * w(n // 16)


def inverse_weight(n):
    def w(i):
        return jnp.where((i == 0) | (i == 3), np.float32(6.0), np.float32(1.2))

    return w(n % 4) * w(n // 4 % 4) * w(n // 16)


def coords():
    me, ev = lax.axis_index("space"), lax.axis_index("event")
    return me, ev, me // 8, me // 2 % 4, me % 2, ev // 2, ev % 2


def copy_to(src, dst, send, recv, **where):
    return pltpu.make_async_remote_copy(
        src_ref=src, dst_ref=dst, send_sem=send, recv_sem=recv, device_id=where, device_id_type=MESH
    )


def signal(barrier, inc=1, **where):
    pl.semaphore_signal(barrier, inc=inc, device_id=where, device_id_type=MESH)


def place_kernel(
    owner_h, ids_h, weights_h, records_h, send_w, send_r,
    owner, ids, weights, records, tail, rows, placed, spots_v, spots, sem, ins,
):
    x = lax.axis_index("event") // 2
    fetch = [
        pltpu.make_async_copy(a, b, ins.at[k])
        for k, (a, b) in enumerate(((owner_h, owner), (ids_h, ids), (records_h, records), (weights_h, weights)))
    ]
    for copy in fetch:
        copy.start()
    fetch[0].wait()
    slab = lax.broadcasted_iota(jnp.int32, (SLABS, 256), 0)
    earlier = (
        lax.broadcasted_iota(jnp.int32, (256, 256), 0) < lax.broadcasted_iota(jnp.int32, (256, 256), 1)
    ).astype(F32).astype(jnp.bfloat16)
    named = [jnp.where(owner[:, 256 * b : 256 * b + 256] == slab, 1.0, 0.0).astype(F32) for b in range(8)]
    counts = jnp.dot(
        jnp.concatenate(named, axis=0).astype(jnp.bfloat16), earlier, preferred_element_type=F32
    )
    carry, found = jnp.zeros((SLABS, 1), F32), []
    for b in range(8):
        rank = jnp.sum(named[b] * (counts[32 * b : 32 * b + 32] + carry), axis=0, keepdims=True)
        carry = carry + jnp.sum(named[b], axis=1, keepdims=True)
        found.append(owner[:, 256 * b : 256 * b + 256] * CAP + rank.astype(jnp.int32))
    for b in range(4):
        spots_v[b : b + 1, :] = found[b] + found[b + 4] * 65536
    copy = pltpu.make_async_copy(spots_v, spots, sem)
    copy.start()
    for k in range(1, 4):
        fetch[k].wait()
    tail[...] = jnp.zeros_like(tail)
    for k in range(4):
        tail[k : k + 1, :] = records[k // 2, k % 2 : k % 2 + 1, :]
    tail[4:5, :] = ids[...].astype(F32)
    for c in range(ST // 128):
        cols = slice(128 * c, 128 * c + 128)
        block = jnp.concatenate(
            [weights[pl.ds(pl.multiple_of((x + q) % 4 * 16, 16), 16), cols] for q in range(DIRECT // 16)]
            + [tail[:, cols], jnp.zeros((120 - DIRECT, 128), F32)],
            axis=0,
        )
        rows[cols, :] = block.T

    def clear(i, carry):
        placed[pl.ds(pl.multiple_of(i * 128, 128), 128), :] = jnp.zeros((128, 128), F32)
        return carry

    lax.fori_loop(0, SLABS * CAP // 128, clear, 0)
    copy.wait()

    def move(i, carry):
        for j in range(16):
            pair = spots[i // 16, i % 16 * 16 + j]
            placed[pl.ds(pair & 65535, 1), :] = rows[pl.ds(i * 16 + j, 1), :]
            placed[pl.ds(pair >> 16, 1), :] = rows[pl.ds(ST // 2 + i * 16 + j, 1), :]
        return carry

    lax.fori_loop(0, ST // 32, move, 0)

    def turn(t, carry):
        for h in range(2):
            block = placed[pl.ds(pl.multiple_of(t * CAP + h * 128, 128), 128), :].T
            send_w[t, :, 128 * h : 128 * h + 128] = block[:DIRECT]
            for r in range(5):
                send_r[t, :, 256 * r + 128 * h : 256 * r + 128 * h + 128] = block[DIRECT + r : DIRECT + r + 1]
        return carry

    lax.fori_loop(0, SLABS, turn, 0)


def place(owner, ids, weights, records):
    return pl.pallas_call(
        place_kernel,
        out_shape=(
            jax.ShapeDtypeStruct((SLABS, DIRECT, CAP), F32),
            jax.ShapeDtypeStruct((SLABS, 1, 5 * CAP), F32),
        ),
        in_specs=[HBM] * 4,
        out_specs=(VM, VM),
        scratch_shapes=[
            pltpu.VMEM((1, ST), jnp.int32),
            pltpu.VMEM((1, ST), jnp.int32),
            pltpu.VMEM((64, ST), F32),
            pltpu.VMEM((2, 2, ST), F32),
            pltpu.VMEM((8, ST), F32),
            pltpu.VMEM((ST, 128), F32),
            pltpu.VMEM((SLABS * CAP, 128), F32),
            pltpu.VMEM((4, 256), jnp.int32),
            pltpu.SMEM((4, 256), jnp.int32),
            DMA,
            DMA((4,)),
        ],
        compiler_params=pltpu.CompilerParams(vmem_limit_bytes=12 << 20),
        name="place",
    )(owner, ids, weights, records)


def weight_goal(dy, dz):
    me, ev, y, z, c, x, half = coords()
    deep = half * 4 + z
    step = (0, 1, 7)[dz] if dz < 3 else 2 + 4 * ((deep // 2 + dy) % 2)
    deep = (deep + step) % 8
    return (y + dy) % 4 * 8 + deep % 4 * 2, x * 2 + deep // 4


def record_goal(dy, dz):
    me, ev, y, z, c, x, half = coords()
    return (y + dy) % 4 * 8 + (z + (0, 1, 3, 2)[dz]) % 4 * 2


def greet_stations(barrier):
    me, ev, y, z, c, x, half = coords()
    for dy in range(4):
        for dz in range(4):
            if dy == 0 and dz == 0:
                signal(barrier, 2, space=me + 1 - 2 * c)
                continue
            goal, event = weight_goal(dy, dz)
            other = record_goal(dy, dz)
            for c2 in range(2):
                signal(barrier, space=goal + c2, event=event)
                signal(barrier, space=other + c2)
    signal(barrier, event=(ev + 2) % 8)
    signal(barrier, event=(ev + 6) % 8)
    return 64


def own_stations(send_w, send_r, got_w, got_r, rw, rr):
    me, ev, y, z, c, x, half = coords()
    here = (0, 0, c)
    pltpu.make_async_copy(send_w.at[me], got_w.at[here], rw.at[here]).start()
    pltpu.make_async_copy(send_r.at[me], got_r.at[here], rr.at[here]).start()


def station_copies(dy, first, send_w, send_r, got_w, got_r, sw, rw, sr, rr):
    me, ev, y, z, c, x, half = coords()
    copies = []
    for dz in range(4):
        for c2 in range(2):
            if first and dz == 0:
                if c2 == 0:
                    continue
                goal = other = me + 1 - 2 * c
                event = ev
            else:
                goal, event = weight_goal(dy, dz)
                goal, other = goal + c2, record_goal(dy, dz) + c2
            mine, there = (dy, dz, c2), (dy, dz, c)
            copies += [
                copy_to(send_w.at[goal], got_w.at[there], sw.at[mine], rw.at[there], space=goal, event=event),
                copy_to(send_r.at[other], got_r.at[there], sr.at[mine], rr.at[there], space=other),
            ]
    return copies


def share_copies(w, got_w, left, right, fs, fr):
    ev = lax.axis_index("event")
    return (
        copy_to(got_w.at[w, :, :, 0:16], left.at[w], fs.at[w, 0], fr.at[w, 0], event=(ev + 2) % 8),
        copy_to(got_w.at[w, :, :, 16:32], right.at[w], fs.at[w, 1], fr.at[w, 1], event=(ev + 6) % 8),
    )


def receive_stations(w, got_w, got_r, left, right, rw, rr, fs, fr):
    for dz in range(4):
        for cs in range(2):
            at = (w, dz, cs)
            pltpu.make_async_copy(got_w.at[at], got_w.at[at], rw.at[at]).wait()
            pltpu.make_async_copy(got_r.at[at], got_r.at[at], rr.at[at]).wait()
    for copy in share_copies(w, got_w, left, right, fs, fr):
        copy.start()


def gather_sources(got_w, got_r, left, right, left_part, onehot, total, receive, start, between, shares):
    def add(w, carry):
        def products(nodes, row, samples, cols):
            for q in range(4):
                product = nodes * samples[:, 256 * q : 256 * q + 256]
                upper = product.astype(jnp.bfloat16)
                at = row + 32 * q
                left_part[at : at + 32, cols] = upper
                left_part[at + 128 : at + 160, cols] = (product - upper.astype(F32)).astype(jnp.bfloat16)

        def direct(k, carry):
            at = (w, k // 2, k % 2)
            cols = pl.ds(pl.multiple_of(k * CAP, CAP), CAP)
            samples = got_r[at]
            products(got_w[at], 0, samples, cols)
            spot = samples[:, 1024:1280].astype(jnp.int32)
            for i in range(8):
                row = lax.broadcasted_iota(jnp.int32, (128, CAP), 0) + 128 * i
                onehot[128 * i : 128 * i + 128, cols] = jnp.where(row == spot, 1.0, 0.0).astype(jnp.bfloat16)
            return carry

        lax.fori_loop(0, 8, direct, 0)

        def shared(k, carry):
            at = (w, k // 2, k % 2)
            cols = pl.ds(pl.multiple_of(k * CAP, CAP), CAP)
            nodes = jnp.concatenate([right[at], left[at]], axis=0)
            products(nodes, 256, got_r[at], cols)
            return carry

        def columns(first, count):
            def body(j, carry):
                at = pl.ds(pl.multiple_of(j * 256, 256), 256)
                part = slice(first, first + count)
                total[j, part] = total[j, part] + lax.dot_general(
                    left_part[part, :], onehot[at, :], (((1,), (1,)), ((), ())), preferred_element_type=F32
                )
                return carry

            lax.fori_loop(0, 4, body, 0)

        @pl.when(w < 3)
        def _():
            receive(w + 1)

        @pl.when(w == 0)
        def _():
            start(3)

        @pl.when(w == 3)
        def _():
            columns(0, 256)

        for copy in shares(w):
            copy.wait_recv()
        lax.fori_loop(0, 8, shared, 0)

        @pl.when(w < 3)
        def _():
            columns(0, 512)

        @pl.when(w == 3)
        def _():
            columns(256, 256)

        between(w)
        return carry

    total[...] = jnp.zeros_like(total)
    lax.fori_loop(0, 4, add, 0)


def spread_sources(total, src):
    x = lax.axis_index("event") // 2

    def tile(i, carry):
        q, r = i // 8, i % 8
        goal = q * 8 + (r // 2 + x) % 4 * 2 + r % 2
        row = r // 4 * 256 + q * 32 + r % 4 * 8
        upper, lower = pl.ds(pl.multiple_of(row, 8), 8), pl.ds(pl.multiple_of(row + 128, 8), 8)
        sums = [total[j, upper, :] + total[j, lower, :] for j in range(4)]
        for j in range(8):
            src[pl.ds(pl.multiple_of(goal * 64 + j * 8, 8), 8), :] = sums[j // 2][:, j % 2 * 128 : j % 2 * 128 + 128]
        return carry

    lax.fori_loop(0, 32, tile, 0)


def row_of(n):
    return n // 8 * 64 + n % 8


def strided(base):
    return pl.ds(base, 8, stride=8)


def tile_of(n):
    return pl.ds(pl.multiple_of(n * 8, 8), 8)


def element_masks():
    sub = lax.broadcasted_iota(jnp.int32, (8, 128), 0)
    lane = lax.broadcasted_iota(jnp.int32, (8, 128), 1)
    return sub, lane


def from_before_x(v):
    sub, lane = element_masks()
    return jnp.where((lane & 15) != 0, pltpu.roll(v, 1, 1), 0.0)


def from_before_y(v):
    sub, lane = element_masks()
    turned = pltpu.roll(v, 16, 1)
    moved = jnp.where(lane < 16, pltpu.roll(turned, 1, 0), turned)
    return jnp.where(((sub & 1) != 0) | (lane >= 16), moved, 0.0)


def after_x(v, old):
    sub, lane = element_masks()
    return jnp.where((lane & 15) != 15, pltpu.roll(v, 127, 1), old)


def after_y(v, old):
    sub, lane = element_masks()
    turned = pltpu.roll(v, 112, 1)
    moved = jnp.where(lane >= 112, pltpu.roll(turned, 7, 0), turned)
    return jnp.where(((sub & 1) != 1) | (lane < 112), moved, old)


def stiffness(now, local, stiff, terms, first, fields=(0, 1, 2, 3)):
    def line(nodes, fresh, fresh_terms):
        mu = [stiff[n] for n in nodes]
        sums = [None] * 4
        for e in range(2):
            g = []
            for f in (e, e + 2):
                if f not in fields and 2 not in fields:
                    continue
                grad = gradient([now[f * 64 + n] for n in nodes])
                g.append(grad)
                if f not in fields:
                    continue
                out = divergence([a * b for a, b in zip(grad, mu)])
                for n, value in zip(nodes, out):
                    local[f * 64 + n] = value if fresh else local[f * 64 + n] + value
            if 2 in fields:
                for i in range(4):
                    pair = g[0][i] * g[1][i]
                    sums[i] = pair if e == 0 else sums[i] + pair
        if 2 in fields:
            for n, value in zip(nodes, sums):
                terms[tile_of(n), :] = value if fresh_terms else terms[tile_of(n), :] + value

    def along_a(l, carry):
        line([4 * l + i for i in range(4)], True, first)
        return carry

    def along_b(l, carry):
        line([l // 4 * 16 + l % 4 + 4 * i for i in range(4)], False, False)
        return carry

    def along_c(l, carry):
        line([l + 16 * i for i in range(4)], False, False)
        return carry

    for body in (along_a, along_b, along_c):
        lax.fori_loop(0, 16, body, 0)


def assemble_xy(local, first, count):
    def along(gap, node_of, from_before, after):
        def lines(i, carry):
            at = [first * 64 + i * 64 + node_of(k) for k in range(16)]
            low, high = [local[n] for n in at], [local[n + gap] for n in at]
            new = [a + from_before(b) for a, b in zip(low, high)]
            end = [after(a, b) for a, b in zip(new, high)]
            for n, a, b in zip(at, new, end):
                local[n] = a
                local[n + gap] = b
            return carry

        lax.fori_loop(0, count, lines, 0)

    along(3, lambda l: 4 * l, from_before_x, after_x)
    along(12, lambda l: l // 4 * 16 + l % 4, from_before_y, after_y)


def pack_faces(local, faces, first, count):
    sub, lane = element_masks()

    def group(i, carry):
        base = i // 4 * 64 + i % 4 * 4
        low = local[base]
        high = pltpu.roll(local[base + 48], 2, 0)
        for q in range(1, 4):
            low = jnp.where((sub >> 1) == q, pltpu.roll(local[base + q], 2 * q, 0), low)
            high = jnp.where((sub >> 1) == q, pltpu.roll(local[base + 48 + q], (2 * q + 2) % 8, 0), high)
        faces[0, i] = low
        faces[1, i] = high
        return carry

    lax.fori_loop(first * 4, first * 4 + count * 4, group, 0)


def assemble_z(local, got, first, count):
    me = lax.axis_index("space")
    sub, lane = element_masks()

    def group(i, carry):
        base = i // 4 * 64 + i % 4 * 4
        before = jnp.where(me > 0, got[0, i], 0.0)
        after = jnp.where(me < SLABS - 1, got[1, i], 0.0)
        for q in range(4):
            low, high = local[base + q], local[base + 48 + q]
            mine = pltpu.roll(before, (8 - 2 * q) % 8, 0) if q else before
            new = low + jnp.where(sub < 2, mine, pltpu.roll(high, 2, 0))
            theirs = pltpu.roll(after, (6 - 2 * q) % 8, 0) if q < 3 else after
            local[base + q] = new
            local[base + 48 + q] = jnp.where(sub < 6, pltpu.roll(new, 6, 0), high + theirs)
        return carry

    lax.fori_loop(first * 4, first * 4 + count * 4, group, 0)


def inverse_mass(density, got, table, inv):
    me = lax.axis_index("space")
    sub, lane = element_masks()

    def planes(v):
        out = []
        low = v + from_before_x(v)
        for a in (low, v, after_x(low, v)):
            new = a + from_before_y(a)
            out += [(new, a, after_y(new, a))]
        return out

    here = planes(density)
    before = planes(jnp.where(me > 0, got[0], 0.0))
    after = planes(jnp.where(me < SLABS - 1, got[1], 0.0))
    for a in range(3):
        for b in range(3):
            v = here[a][b]
            low = v + jnp.where(sub < 2, pltpu.roll(before[a][b], 2, 0), pltpu.roll(v, 2, 0))
            high = v + jnp.where(sub < 6, pltpu.roll(v, 6, 0), pltpu.roll(after[a][b], 6, 0))
            for c, value in enumerate((low, v, high)):
                table[9 * c + 3 * b + a] = 1.0 / value

    def node(n, carry):
        def part(i):
            return (i + 1) // 2

        at = part(n // 16) * 9 + part(n // 4 % 4) * 3 + part(n % 4)
        inv[n] = table[at] * (inverse_weight(n) * np.float32(STEP_SQUARE))
        return carry

    lax.fori_loop(0, 64, node, 0)


def step_kernel(
    send_w, send_r, fwd_now_h, fwd_prev_h, adj_now_h, adj_prev_h, shear_h, density,
    fwd_last, fwd_before, adj_last, adj_before, pieces,
    fwd_now, fwd_prev, adj_now, adj_prev, shear,
    got_w, got_r, left, right, left_part, onehot, total, src,
    zero, one, local, stiff, inv, table, terms, faces, got_faces, got_density, out_terms,
    sw, rw, sr, rr, fs, fr, hs, hr, ds, dr, ts, tr, ins,
):
    pairs = (
        (fwd_now_h, fwd_now), (adj_now_h, adj_now), (shear_h, shear), (fwd_prev_h, fwd_prev), (adj_prev_h, adj_prev)
    )
    fetch = [pltpu.make_async_copy(a, b, ins.at[k]) for k, (a, b) in enumerate(pairs)]
    for copy in fetch:
        copy.start()
    me, ev, y, z, c, x, half = coords()
    up, down = (me + 1) % SLABS, (me + SLABS - 1) % SLABS
    barrier = pltpu.get_barrier_semaphore()
    greeted = greet_stations(barrier)
    for k in range(1, EVENT):
        signal(barrier, event=(ev + k) % EVENT)
    signal(barrier, space=up)
    signal(barrier, space=down)

    pl.semaphore_wait(barrier, greeted + EVENT - 1 + 2)

    weigh = [
        copy_to(density, got_density.at[1], ds.at[1], dr.at[1], space=down),
        copy_to(density, got_density.at[0], ds.at[0], dr.at[0], space=up),
    ]
    for copy in weigh:
        copy.start()
    stations = (send_w, send_r, got_w, got_r, sw, rw, sr, rr)

    def start(w):
        for copy in station_copies(w, False, *stations):
            copy.start()

    def receive(w):
        receive_stations(w, got_w, got_r, left, right, rw, rr, fs, fr)

    def shares(w):
        return share_copies(w, got_w, left, right, fs, fr)

    first_wave = station_copies(0, True, *stations)
    for copy in first_wave:
        copy.start()
    own_stations(send_w, send_r, got_w, got_r, rw, rr)
    start(1)

    for copy in fetch:
        copy.wait()

    def load(n, carry):
        for f, ref in enumerate((fwd_now, adj_now)):
            for e in range(2):
                zero[(2 * f + e) * 64 + n] = ref[strided(e * 512 + row_of(n)), :]
        stiff[n] = shear[strided(row_of(n)), :] * node_weight(n)
        return carry

    lax.fori_loop(0, 64, load, 0)

    def exchange(step, first, count):
        assemble_xy(local, first, count)
        pack_faces(local, faces.at[step], first, count)
        at, k = slice(first * 4, first * 4 + count * 4), first // 2
        halo = [
            copy_to(faces.at[step, 0, at], got_faces.at[step, 1, at], hs.at[step, k, 0], hr.at[step, k, 0], space=down),
            copy_to(faces.at[step, 1, at], got_faces.at[step, 0, at], hs.at[step, k, 1], hr.at[step, k, 1], space=up),
        ]
        for copy in halo:
            copy.start()
        return halo

    def advance(step, first, count):
        assemble_z(local, got_faces.at[step], first, count)

        def update(n, carry):
            mine = inv[n]
            for f in range(first, first + count):
                at, row = f * 64 + n, strided(f % 2 * 512 + row_of(n))
                if step == 0:
                    old = (fwd_prev, adj_prev)[f // 2][row, :]
                    new = 2.0 * zero[at] - old - local[at] * mine
                    one[at] = new
                    (fwd_before, adj_before)[f // 2][row, :] = new
                else:
                    (fwd_last, adj_last)[f // 2][row, :] = 2.0 * one[at] - zero[at] - local[at] * mine
            return carry

        lax.fori_loop(0, 64, update, 0)

    def subtract(step):
        def less(n, carry):
            for e in range(2):
                at = (2 + e) * 64 + n
                local[at] = local[at] - src[strided((2 * e + step) * 512 + row_of(n)), :]
            return carry

        lax.fori_loop(0, 64, less, 0)

    stiffness(zero, local, stiff, terms, True)
    receive(0)
    start(2)
    forward = exchange(0, 0, 2)

    def between(w):
        @pl.when(w == 0)
        def _():
            for copy in weigh:
                copy.wait_recv()
            inverse_mass(density[...], got_density, table, inv)

        @pl.when(w == 2)
        def _():
            for copy in forward:
                copy.wait_recv()
            advance(0, 0, 2)
            stiffness(one, local, stiff, terms, False, (0, 1))

    gather_sources(got_w, got_r, left, right, left_part, onehot, total, receive, start, between, shares)
    spread_sources(total, src)
    subtract(0)
    adjoint = exchange(0, 2, 2)
    forward_last = exchange(1, 0, 2)
    for copy in adjoint:
        copy.wait_recv()
    advance(0, 2, 2)

    stiffness(one, local, stiff, terms, False, (2, 3))

    def cut(j, carry):
        out_terms[j] = terms[pl.ds(j, 64, stride=8), :]
        return carry

    lax.fori_loop(0, EVENT, cut, 0)
    given = []
    for k in range(1, EVENT):
        goal = (ev + k) % EVENT
        given.append(copy_to(out_terms.at[goal], pieces.at[k], ts.at[k], tr.at[k], event=goal))
    for copy in given:
        copy.start()
    subtract(1)
    adjoint_last = exchange(1, 2, 2)
    pieces[0] = out_terms[ev]
    for copy in forward_last:
        copy.wait_recv()
    advance(1, 0, 2)
    for copy in adjoint_last:
        copy.wait_recv()
    advance(1, 2, 2)
    for copy in given:
        copy.wait_recv()

    for copy in first_wave + weigh + forward + adjoint + forward_last + adjoint_last + given:
        copy.wait_send()

    def last(w, carry):
        for copy in station_copies(w, False, *stations):
            copy.wait_send()
        return carry

    lax.fori_loop(1, 4, last, 0)

    def last_shares(w, carry):
        for copy in shares(w):
            copy.wait_send()
        return carry

    lax.fori_loop(0, 4, last_shares, 0)


def steps(send_w, send_r, fwd_now, fwd_prev, adj_now, adj_prev, shear, density):
    fields = pltpu.VMEM((256, 8, 128), F32)
    waves = DMA((4, 4, 2))
    return pl.pallas_call(
        step_kernel,
        out_shape=(
            *[jax.ShapeDtypeStruct((1024, 128), F32)] * 4,
            jax.ShapeDtypeStruct((EVENT, 64, 128), F32),
        ),
        in_specs=[VM, VM, HBM, HBM, HBM, HBM, HBM, VM],
        out_specs=(VM,) * 5,
        scratch_shapes=[
            *[pltpu.VMEM((1024, 128), F32)] * 4,
            pltpu.VMEM((512, 128), F32),
            pltpu.VMEM((4, 4, 2, DIRECT, CAP), F32),
            pltpu.VMEM((4, 4, 2, 1, 5 * CAP), F32),
            pltpu.VMEM((4, 4, 2, 16, CAP), F32),
            pltpu.VMEM((4, 4, 2, 16, CAP), F32),
            pltpu.VMEM((512, 8 * CAP), jnp.bfloat16),
            pltpu.VMEM((ELEMS, 8 * CAP), jnp.bfloat16),
            pltpu.VMEM((4, 512, 256), F32),
            pltpu.VMEM((2048, 128), F32),
            fields,
            fields,
            fields,
            pltpu.VMEM((64, 8, 128), F32),
            pltpu.VMEM((64, 8, 128), F32),
            pltpu.VMEM((27, 8, 128), F32),
            pltpu.VMEM((512, 128), F32),
            pltpu.VMEM((2, 2, 16, 8, 128), F32),
            pltpu.VMEM((2, 2, 16, 8, 128), F32),
            pltpu.VMEM((2, 8, 128), F32),
            pltpu.VMEM((EVENT, 64, 128), F32),
            waves, waves, waves, waves,
            DMA((4, 2)), DMA((4, 2)),
            DMA((2, 2, 2)), DMA((2, 2, 2)),
            DMA((2,)), DMA((2,)),
            DMA((EVENT,)), DMA((EVENT,)),
            DMA((5,)),
        ],
        compiler_params=pltpu.CompilerParams(collective_id=0, has_side_effects=True, vmem_limit_bytes=32 << 20),
        name="steps",
    )(send_w, send_r, fwd_now, fwd_prev, adj_now, adj_prev, shear, density)


def finish_kernel(a, b, c, d, pieces, shear, a_out, b_out, c_out, d_out, kernel_out, kernel, sems):
    ev = lax.axis_index("event")
    copies = [
        pltpu.make_async_copy(src, dst, sems.at[k])
        for k, (src, dst) in enumerate(((a, a_out), (b, b_out), (c, c_out), (d, d_out), (kernel, kernel_out)))
    ]
    for copy in copies[:4]:
        copy.start()
    for i in range(8):
        rows = slice(8 * i, 8 * i + 8)
        total = pieces[0, rows]
        for k in range(1, EVENT):
            total = total + pieces[k, rows]
        n = 8 * i + lax.broadcasted_iota(jnp.int32, (8, 128), 0)
        edge = [((n >> 2 * k) & 3) * (3 - ((n >> 2 * k) & 3)) == 0 for k in range(3)]
        weight = [jnp.where(e, np.float32(1.0 / 6.0), np.float32(5.0 / 6.0)) for e in edge]
        factor = weight[0] * weight[1] * weight[2] * np.float32(-TIME_STEP)
        kernel[rows, :] = total * (factor * shear[pl.ds(pl.multiple_of(i * 64 + ev * 8, 8), 8), :])
    copies[4].start()
    for copy in copies:
        copy.wait()


def finish(*given):
    return pl.pallas_call(
        finish_kernel,
        out_shape=(*[jax.ShapeDtypeStruct((1024, 128), F32)] * 4, jax.ShapeDtypeStruct((64, 128), F32)),
        in_specs=[VM] * 6,
        out_specs=(HBM,) * 5,
        scratch_shapes=[pltpu.VMEM((64, 128), F32), DMA((5,))],
        compiler_params=pltpu.CompilerParams(vmem_limit_bytes=8 << 20),
        name="finish",
    )(*given)


def to_rows(field):
    count = field.size // (64 * ELEMS)
    return field.reshape(count, 8, 8, 8, 128).transpose(0, 1, 3, 2, 4).reshape(count * 512, 128)


def from_rows(rows):
    return rows.reshape(2, 8, 8, 8, 128).transpose(0, 1, 3, 2, 4).reshape(2, 64, ELEMS)


def shards(
    fwd_now, fwd_prev, adj_now, adj_prev, shear_mod, density, station_owner, receiver_local, station_weights, adj_records
):
    def far(value):
        return pltpu.with_memory_space_constraint(value, pltpu.HBM)

    shear = to_rows(shear_mod)
    send_w, send_r = place(
        far(station_owner.T), far(receiver_local.reshape(1, ST)), far(station_weights), far(adj_records)
    )
    found = steps(
        send_w, send_r, *[far(to_rows(v)) for v in (fwd_now, fwd_prev, adj_now, adj_prev)],
        shear, density.reshape(8, 128),
    )
    *fields, kernel = finish(*found, shear)
    return (*map(from_rows, fields), kernel)


def solution(mesh):
    fields = P("event", None, "space")
    return jax.shard_map(
        shards,
        mesh=mesh,
        in_specs=(
            fields, fields, fields, fields,
            P(None, "space"), P("space"), P("space", None), P("space"), P(None, "space"), fields,
        ),
        out_specs=(fields, fields, fields, fields, P(None, ("space", "event"))),
        check_vma=False,
    )
```

time: 125 us -> 78.6 us (0.63)
  Pallas kernels: 115 us -> 77.8 us
  local copies, waits for them, and re-layouts: 7.25 us -> 0.01 us
  other arithmetic: 1.36 us -> 0 us
    pallas_call x1, Pallas kernels: 103 us -> 67.9 us  [steps(): pl.pallas_call(step_kernel, out_shape=(*[jax.ShapeDtypeStruct((1024, 128)...]
    unnamed x19 -> x4, local copies, waits for them, and re-layouts: 7.24 us -> 0.01 us
    unnamed x1 -> x0, other arithmetic: 1.36 us -> none
    pallas_call x1, Pallas kernels: 9.88 us -> 8.55 us  [place(): pl.pallas_call(place_kernel, out_shape=(jax.ShapeDtypeStruct((SLABS, DIRE...]
where the time goes in v1:
time: 78.6 us; the launch traced here: 78.5 us
  Pallas kernels  77.8 us (99%)
    pallas_call x1, Pallas kernels, steps(): pl.pallas_call(step_kernel, out_shape=(*[jax.ShapeDtypeStruct((1024, 128)...  67.9 us
    pallas_call x1, Pallas kernels, place(): pl.pallas_call(place_kernel, out_shape=(jax.ShapeDtypeStruct((SLABS, DIRE...  8.55 us

profile of v1, /device:TPU:2, one launch (start us, length us, event | category | flops | bytes accessed | tf_op | source)
XLA Modules:
  0.0 78.5 jit_solution(8411515577311593322)
XLA Ops:
  0.6 0.0 copy-start
  0.6 0.0 copy-start.1
  0.7 8.6 %place.1 = (f32[32,32,256]{2,1,0:T(8,128)S(1)}, f32[32,1,1280]{2,1,0:T(1,128)S(1)}) custom-call(s32[1,2048]{1,0:T(1,128)} %bitcast.55, s32[1,2048]{1,0:T(1,128)} %bitcast.56, f32[64,2048]{1,0:T(8,128)} %weights_h.1, f32[2,2,2048]{2,1,0:T(2,128)} %records_h.1), custom_call_target="tpu_custom_call" | custom-call | tf_op jit(solution)/shard_map/place/pallas_call | solution.py:155
  9.2 0.0 copy-done
  9.2 0.0 copy-done.1
  9.2 67.9 %steps.1 = (f32[1024,128]{1,0:T(8,128)S(1)}, f32[1024,128]{1,0:T(8,128)S(1)}, f32[1024,128]{1,0:T(8,128)S(1)}, f32[1024,128]{1,0:T(8,128)S(1)}, f32[8,64,128]{2,1,0:T(8,128)S(1)}) custom-call(f32[32,32,256]{2,1,0:T(8,128)S(1)} %get-tuple-element.17.send_w, f32[32,1,1280]{2,1,0:T(1,128)S(1)} %get-tuple-element.18.send_r, f32[1024,128]{1,0:T(8,128)} %bitcast.51, ...), custom_call_target="tpu_custom_call" | custom-call | tf_op jit(solution)/shard_map/steps/pallas_call | solution.py:690
  77.2 1.4 %finish.1 = (f32[1024,128]{1,0:T(8,128)}, f32[1024,128]{1,0:T(8,128)}, f32[1024,128]{1,0:T(8,128)}, f32[1024,128]{1,0:T(8,128)}, f32[64,128]{1,0:T(8,128)}) custom-call(f32[1024,128]{1,0:T(8,128)S(1)} %get-tuple-element.19.a, f32[1024,128]{1,0:T(8,128)S(1)} %get-tuple-element.20.b, f32[1024,128]{1,0:T(8,128)S(1)} %get-tuple-element.21.c, ...), custom_call_target="tpu_custom_call" | custom-call | tf_op jit(solution)/shard_map/finish/pallas_call | solution.py:756
Async XLA Ops:
  0.6 8.6 %copy-start = (f32[64,1024]{1,0:T(8,128)S(1)}, f32[64,1024]{1,0:T(8,128)}, u32[]{:S(2)}) copy-start(f32[64,1024]{1,0:T(8,128)} %param.14) | copy-start | bytes 786436
  0.6 8.6 %copy-start.1 = (f32[1024]{0:T(1024)S(1)}, f32[1024]{0:T(1024)}, u32[]{:S(2)}) copy-start(f32[1024]{0:T(1024)} %param.15) | copy-start | bytes 12292

commit v2 on v1

--- a/solution.py
+++ b/solution.py
@@ -51,18 +51,8 @@
     return [r + q0, q1 - r, -q1 - r, r - q0]
 
 
-def node_weight(n):
-    def w(i):
-        return jnp.where((i == 0) | (i == 3), np.float32(1.0 / 6.0), np.float32(5.0 / 6.0))
-
-    return w(n % 4) * w(n // 4 % 4) * w(n // 16)
-
-
-def inverse_weight(n):
-    def w(i):
-        return jnp.where((i == 0) | (i == 3), np.float32(6.0), np.float32(1.2))
-
-    return w(n % 4) * w(n // 4 % 4) * w(n // 16)
+def point_weight(i):
+    return jnp.where((i == 0) | (i == 3), np.float32(1.0 / 6.0), np.float32(5.0 / 6.0))
 
 
 def coords():
@@ -254,7 +244,7 @@
         copy.start()
 
 
-def gather_sources(got_w, got_r, left, right, left_part, onehot, total, receive, start, between, shares):
+def gather_sources(got_w, got_r, left, right, left_part, onehot, total, receive, start, shares):
     def add(w, carry):
         def products(nodes, row, samples, cols):
             for q in range(4):
@@ -319,7 +309,6 @@
         def _():
             columns(256, 256)
 
-        between(w)
         return carry
 
     total[...] = jnp.zeros_like(total)
@@ -352,6 +341,15 @@
 
 def tile_of(n):
     return pl.ds(pl.multiple_of(n * 8, 8), 8)
+
+
+def each_node(body):
+    def group(g, carry):
+        for r in range(8):
+            body(g * 8 + r, g * 64 + r)
+        return carry
+
+    lax.fori_loop(0, 8, group, 0)
 
 
 def element_masks():
@@ -479,7 +477,7 @@
     lax.fori_loop(first * 4, first * 4 + count * 4, group, 0)
 
 
-def inverse_mass(density, got, table, inv):
+def inverse_mass(density, got, inv):
     me = lax.axis_index("space")
     sub, lane = element_masks()
 
@@ -500,17 +498,12 @@
             low = v + jnp.where(sub < 2, pltpu.roll(before[a][b], 2, 0), pltpu.roll(v, 2, 0))
             high = v + jnp.where(sub < 6, pltpu.roll(v, 6, 0), pltpu.roll(after[a][b], 6, 0))
             for c, value in enumerate((low, v, high)):
-                table[9 * c + 3 * b + a] = 1.0 / value
-
-    def node(n, carry):
-        def part(i):
-            return (i + 1) // 2
-
-        at = part(n // 16) * 9 + part(n // 4 % 4) * 3 + part(n % 4)
-        inv[n] = table[at] * (inverse_weight(n) * np.float32(STEP_SQUARE))
-        return carry
-
-    lax.fori_loop(0, 64, node, 0)
+                inverse = 1.0 / value
+                for n in range(64):
+                    at = n % 4, n // 4 % 4, n // 16
+                    if tuple((i + 1) // 2 for i in at) == (a, b, c):
+                        weight = np.prod([1.2 if i in (1, 2) else 6.0 for i in at])
+                        inv[n] = inverse * np.float32(STEP_SQUARE * weight)
 
 
 def step_kernel(
@@ -518,7 +511,7 @@
     fwd_last, fwd_before, adj_last, adj_before, pieces,
     fwd_now, fwd_prev, adj_now, adj_prev, shear,
     got_w, got_r, left, right, left_part, onehot, total, src,
-    zero, one, local, stiff, inv, table, terms, faces, got_faces, got_density, out_terms,
+    zero, one, local, stiff, inv, terms, faces, got_faces, got_density, out_terms, got_terms,
     sw, rw, sr, rr, fs, fr, hs, hr, ds, dr, ts, tr, ins,
 ):
     pairs = (
@@ -531,12 +524,13 @@
     up, down = (me + 1) % SLABS, (me + SLABS - 1) % SLABS
     barrier = pltpu.get_barrier_semaphore()
     greeted = greet_stations(barrier)
-    for k in range(1, EVENT):
-        signal(barrier, event=(ev + k) % EVENT)
+    for k in range(1, 4):
+        signal(barrier, event=(ev + 2 * k) % EVENT)
+    signal(barrier, event=x * 2 + 1 - half)
     signal(barrier, space=up)
     signal(barrier, space=down)
 
-    pl.semaphore_wait(barrier, greeted + EVENT - 1 + 2)
+    pl.semaphore_wait(barrier, greeted + 4 + 2)
 
     weigh = [
         copy_to(density, got_density.at[1], ds.at[1], dr.at[1], space=down),
@@ -565,14 +559,17 @@
     for copy in fetch:
         copy.wait()
 
-    def load(n, carry):
-        for f, ref in enumerate((fwd_now, adj_now)):
-            for e in range(2):
-                zero[(2 * f + e) * 64 + n] = ref[strided(e * 512 + row_of(n)), :]
-        stiff[n] = shear[strided(row_of(n)), :] * node_weight(n)
-        return carry
-
-    lax.fori_loop(0, 64, load, 0)
+    def load(g, carry):
+        for r in range(8):
+            n, row = g * 8 + r, g * 64 + r
+            for f, ref in enumerate((fwd_now, adj_now)):
+                for e in range(2):
+                    zero[(2 * f + e) * 64 + n] = ref[strided(e * 512 + row), :]
+            along_a = np.float32((1.0 / 6.0, 5.0 / 6.0, 5.0 / 6.0, 1.0 / 6.0)[r % 4])
+            stiff[n] = shear[strided(row), :] * (point_weight((2 * g + r // 4) % 4) * point_weight(g // 2) * along_a)
+        return carry
+
+    lax.fori_loop(0, 8, load, 0)
 
     def exchange(step, first, count):
         assemble_xy(local, first, count)
@@ -589,58 +586,50 @@
     def advance(step, first, count):
         assemble_z(local, got_faces.at[step], first, count)
 
-        def update(n, carry):
+        def update(n, row):
             mine = inv[n]
             for f in range(first, first + count):
-                at, row = f * 64 + n, strided(f % 2 * 512 + row_of(n))
+                at, rows = f * 64 + n, strided(f % 2 * 512 + row)
                 if step == 0:
-                    old = (fwd_prev, adj_prev)[f // 2][row, :]
+                    old = (fwd_prev, adj_prev)[f // 2][rows, :]
                     new = 2.0 * zero[at] - old - local[at] * mine
                     one[at] = new
-                    (fwd_before, adj_before)[f // 2][row, :] = new
+                    (fwd_before, adj_before)[f // 2][rows, :] = new
                 else:
-                    (fwd_last, adj_last)[f // 2][row, :] = 2.0 * one[at] - zero[at] - local[at] * mine
-            return carry
-
-        lax.fori_loop(0, 64, update, 0)
+                    (fwd_last, adj_last)[f // 2][rows, :] = 2.0 * one[at] - zero[at] - local[at] * mine
+
+        each_node(update)
 
     def subtract(step):
-        def less(n, carry):
+        def less(n, row):
             for e in range(2):
                 at = (2 + e) * 64 + n
-                local[at] = local[at] - src[strided((2 * e + step) * 512 + row_of(n)), :]
-            return carry
-
-        lax.fori_loop(0, 64, less, 0)
+                local[at] = local[at] - src[strided((2 * e + step) * 512 + row), :]
+
+        each_node(less)
+
+    def arrived(copies):
+        for copy in copies:
+            copy.wait_recv()
 
     stiffness(zero, local, stiff, terms, True)
+    forward = exchange(0, 0, 2)
+    arrived(weigh)
+    inverse_mass(density[...], got_density, inv)
     receive(0)
     start(2)
-    forward = exchange(0, 0, 2)
-
-    def between(w):
-        @pl.when(w == 0)
-        def _():
-            for copy in weigh:
-                copy.wait_recv()
-            inverse_mass(density[...], got_density, table, inv)
-
-        @pl.when(w == 2)
-        def _():
-            for copy in forward:
-                copy.wait_recv()
-            advance(0, 0, 2)
-            stiffness(one, local, stiff, terms, False, (0, 1))
-
-    gather_sources(got_w, got_r, left, right, left_part, onehot, total, receive, start, between, shares)
+    gather_sources(got_w, got_r, left, right, left_part, onehot, total, receive, start, shares)
     spread_sources(total, src)
     subtract(0)
     adjoint = exchange(0, 2, 2)
+
+    arrived(forward)
+    advance(0, 0, 2)
+    stiffness(one, local, stiff, terms, False, (0, 1))
     forward_last = exchange(1, 0, 2)
-    for copy in adjoint:
-        copy.wait_recv()
+
+    arrived(adjoint)
     advance(0, 2, 2)
-
     stiffness(one, local, stiff, terms, False, (2, 3))
 
     def cut(j, carry):
@@ -649,22 +638,27 @@
 
     lax.fori_loop(0, EVENT, cut, 0)
     given = []
-    for k in range(1, EVENT):
-        goal = (ev + k) % EVENT
-        given.append(copy_to(out_terms.at[goal], pieces.at[k], ts.at[k], tr.at[k], event=goal))
-    for copy in given:
-        copy.start()
+    for k in range(1, 4):
+        goal = (x + k) % 4 * 2
+        given.append(
+            copy_to(out_terms.at[pl.ds(goal, 2)], got_terms.at[k], ts.at[k], tr.at[k], event=goal + half)
+        )
+        given[-1].start()
     subtract(1)
     adjoint_last = exchange(1, 2, 2)
-    pieces[0] = out_terms[ev]
-    for copy in forward_last:
-        copy.wait_recv()
+    arrived(forward_last)
     advance(1, 0, 2)
-    for copy in adjoint_last:
-        copy.wait_recv()
+
+    arrived(given)
+    for h in range(2):
+        got_terms[0, h] = out_terms[x * 2 + h] + got_terms[1, h] + got_terms[2, h] + got_terms[3, h]
+    other = copy_to(got_terms.at[0, 1 - half], pieces.at[1], ts.at[0], tr.at[0], event=x * 2 + 1 - half)
+    other.start()
+    pieces[0] = got_terms[0, half]
+    arrived(adjoint_last)
     advance(1, 2, 2)
-    for copy in given:
-        copy.wait_recv()
+    other.wait_recv()
+    given.append(other)
 
     for copy in first_wave + weigh + forward + adjoint + forward_last + adjoint_last + given:
         copy.wait_send()
@@ -691,7 +685,7 @@
         step_kernel,
         out_shape=(
             *[jax.ShapeDtypeStruct((1024, 128), F32)] * 4,
-            jax.ShapeDtypeStruct((EVENT, 64, 128), F32),
+            jax.ShapeDtypeStruct((2, 64, 128), F32),
         ),
         in_specs=[VM, VM, HBM, HBM, HBM, HBM, HBM, VM],
         out_specs=(VM,) * 5,
@@ -711,17 +705,17 @@
             fields,
             pltpu.VMEM((64, 8, 128), F32),
             pltpu.VMEM((64, 8, 128), F32),
-            pltpu.VMEM((27, 8, 128), F32),
             pltpu.VMEM((512, 128), F32),
             pltpu.VMEM((2, 2, 16, 8, 128), F32),
             pltpu.VMEM((2, 2, 16, 8, 128), F32),
             pltpu.VMEM((2, 8, 128), F32),
             pltpu.VMEM((EVENT, 64, 128), F32),
+            pltpu.VMEM((4, 2, 64, 128), F32),
             waves, waves, waves, waves,
             DMA((4, 2)), DMA((4, 2)),
             DMA((2, 2, 2)), DMA((2, 2, 2)),
             DMA((2,)), DMA((2,)),
-            DMA((EVENT,)), DMA((EVENT,)),
+            DMA((4,)), DMA((4,)),
             DMA((5,)),
         ],
         compiler_params=pltpu.CompilerParams(collective_id=0, has_side_effects=True, vmem_limit_bytes=32 << 20),
@@ -739,9 +733,7 @@
         copy.start()
     for i in range(8):
         rows = slice(8 * i, 8 * i + 8)
-        total = pieces[0, rows]
-        for k in range(1, EVENT):
-            total = total + pieces[k, rows]
+        total = pieces[0, rows] + pieces[1, rows]
         n = 8 * i + lax.broadcasted_iota(jnp.int32, (8, 128), 0)
         edge = [((n >> 2 * k) & 3) * (3 - ((n >> 2 * k) & 3)) == 0 for k in range(3)]
         weight = [jnp.where(e, np.float32(1.0 / 6.0), np.float32(5.0 / 6.0)) for e in edge]

time: 78.6 us -> 73.3 us (0.933)
  Pallas kernels: 77.8 us -> 72.5 us
    pallas_call x1, Pallas kernels: 67.9 us -> 62.6 us  [steps(): pl.pallas_call(step_kernel, out_shape=(*[jax.ShapeDtypeStruct((1024, 128)...]
where the time goes in v2:
time: 73.3 us; the launch traced here: 73.2 us
  Pallas kernels  72.5 us (99%)
    pallas_call x1, Pallas kernels, steps(): pl.pallas_call(step_kernel, out_shape=(*[jax.ShapeDtypeStruct((1024, 128)...  62.6 us
    pallas_call x1, Pallas kernels, place(): pl.pallas_call(place_kernel, out_shape=(jax.ShapeDtypeStruct((SLABS, DIRE...  8.55 us

profile of v2, /device:TPU:2, one launch (start us, length us, event | category | flops | bytes accessed | tf_op | source)
XLA Modules:
  0.0 73.2 jit_solution(17757624387499027554)
XLA Ops:
  0.6 0.0 copy-start
  0.6 0.0 copy-start.1
  0.7 8.6 %place.1 = (f32[32,32,256]{2,1,0:T(8,128)S(1)}, f32[32,1,1280]{2,1,0:T(1,128)S(1)}) custom-call(s32[1,2048]{1,0:T(1,128)} %bitcast.55, s32[1,2048]{1,0:T(1,128)} %bitcast.56, f32[64,2048]{1,0:T(8,128)} %weights_h.1, f32[2,2,2048]{2,1,0:T(2,128)} %records_h.1), custom_call_target="tpu_custom_call" | custom-call | tf_op jit(solution)/shard_map/place/pallas_call | solution.py:145
  9.2 0.0 copy-done
  9.2 0.0 copy-done.1
  9.2 62.6 %steps.1 = (f32[1024,128]{1,0:T(8,128)S(1)}, f32[1024,128]{1,0:T(8,128)S(1)}, f32[1024,128]{1,0:T(8,128)S(1)}, f32[1024,128]{1,0:T(8,128)S(1)}, f32[2,64,128]{2,1,0:T(8,128)S(1)}) custom-call(f32[32,32,256]{2,1,0:T(8,128)S(1)} %get-tuple-element.17.send_w, f32[32,1,1280]{2,1,0:T(1,128)S(1)} %get-tuple-element.18.send_r, f32[1024,128]{1,0:T(8,128)} %bitcast.51, ...), custom_call_target="tpu_custom_call" | custom-call | tf_op jit(solution)/shard_map/steps/pallas_call | solution.py:684
  71.8 1.4 %finish.1 = (f32[1024,128]{1,0:T(8,128)}, f32[1024,128]{1,0:T(8,128)}, f32[1024,128]{1,0:T(8,128)}, f32[1024,128]{1,0:T(8,128)}, f32[64,128]{1,0:T(8,128)}) custom-call(f32[1024,128]{1,0:T(8,128)S(1)} %get-tuple-element.19.a, f32[1024,128]{1,0:T(8,128)S(1)} %get-tuple-element.20.b, f32[1024,128]{1,0:T(8,128)S(1)} %get-tuple-element.21.c, ...), custom_call_target="tpu_custom_call" | custom-call | tf_op jit(solution)/shard_map/finish/pallas_call | solution.py:748
Async XLA Ops:
  0.6 8.6 %copy-start = (f32[64,1024]{1,0:T(8,128)S(1)}, f32[64,1024]{1,0:T(8,128)}, u32[]{:S(2)}) copy-start(f32[64,1024]{1,0:T(8,128)} %param.14) | copy-start | bytes 786436
  0.6 8.6 %copy-start.1 = (f32[1024]{0:T(1024)S(1)}, f32[1024]{0:T(1024)}, u32[]{:S(2)}) copy-start(f32[1024]{0:T(1024)} %param.15) | copy-start | bytes 12292

commit v3 on v2

--- a/solution.py
+++ b/solution.py
@@ -13,6 +13,7 @@
 F32 = jnp.float32
 SLABS, EVENT, CAP, ST, ELEMS = 32, 8, 256, 2048, 1024
 DIRECT = 32
+EARLY = 4
 TIME_STEP, STEP_SQUARE = 0.08, 0.0064
 
 
@@ -71,8 +72,8 @@
 
 
 def place_kernel(
-    owner_h, ids_h, weights_h, records_h, send_w, send_r,
-    owner, ids, weights, records, tail, rows, placed, spots_v, spots, sem, ins,
+    owner_h, ids_h, weights_h, records_h, placed,
+    owner, ids, weights, records, tail, rows, spots_v, spots, sem, ins,
 ):
     x = lax.axis_index("event") // 2
     fetch = [
@@ -130,26 +131,13 @@
 
     lax.fori_loop(0, ST // 32, move, 0)
 
-    def turn(t, carry):
-        for h in range(2):
-            block = placed[pl.ds(pl.multiple_of(t * CAP + h * 128, 128), 128), :].T
-            send_w[t, :, 128 * h : 128 * h + 128] = block[:DIRECT]
-            for r in range(5):
-                send_r[t, :, 256 * r + 128 * h : 256 * r + 128 * h + 128] = block[DIRECT + r : DIRECT + r + 1]
-        return carry
-
-    lax.fori_loop(0, SLABS, turn, 0)
-
 
 def place(owner, ids, weights, records):
     return pl.pallas_call(
         place_kernel,
-        out_shape=(
-            jax.ShapeDtypeStruct((SLABS, DIRECT, CAP), F32),
-            jax.ShapeDtypeStruct((SLABS, 1, 5 * CAP), F32),
-        ),
+        out_shape=jax.ShapeDtypeStruct((SLABS * CAP, 128), F32),
         in_specs=[HBM] * 4,
-        out_specs=(VM, VM),
+        out_specs=VM,
         scratch_shapes=[
             pltpu.VMEM((1, ST), jnp.int32),
             pltpu.VMEM((1, ST), jnp.int32),
@@ -157,7 +145,6 @@
             pltpu.VMEM((2, 2, ST), F32),
             pltpu.VMEM((8, ST), F32),
             pltpu.VMEM((ST, 128), F32),
-            pltpu.VMEM((SLABS * CAP, 128), F32),
             pltpu.VMEM((4, 256), jnp.int32),
             pltpu.SMEM((4, 256), jnp.int32),
             DMA,
@@ -166,6 +153,26 @@
         compiler_params=pltpu.CompilerParams(vmem_limit_bytes=12 << 20),
         name="place",
     )(owner, ids, weights, records)
+
+
+def wave_shift(w):
+    return w + w // 2 - 2 * (w // 3)
+
+
+def turn_stations(w, placed, send_w, send_r):
+    me, ev, y, z, c, x, half = coords()
+    base = (y + wave_shift(w)) % 4 * 8
+
+    def block(t, carry):
+        slab = base + t
+        for h in range(2):
+            turned = placed[pl.ds(pl.multiple_of(slab * CAP + h * 128, 128), 128), :].T
+            send_w[slab, :, 128 * h : 128 * h + 128] = turned[:DIRECT]
+            for r in range(5):
+                send_r[slab, :, 256 * r + 128 * h : 256 * r + 128 * h + 128] = turned[DIRECT + r : DIRECT + r + 1]
+        return carry
+
+    lax.fori_loop(0, 8, block, 0)
 
 
 def weight_goal(dy, dz):
@@ -205,7 +212,7 @@
     pltpu.make_async_copy(send_r.at[me], got_r.at[here], rr.at[here]).start()
 
 
-def station_copies(dy, first, send_w, send_r, got_w, got_r, sw, rw, sr, rr):
+def station_copies(w, first, send_w, send_r, got_w, got_r, sw, rw, sr, rr):
     me, ev, y, z, c, x, half = coords()
     copies = []
     for dz in range(4):
@@ -216,9 +223,9 @@
                 goal = other = me + 1 - 2 * c
                 event = ev
             else:
-                goal, event = weight_goal(dy, dz)
-                goal, other = goal + c2, record_goal(dy, dz) + c2
-            mine, there = (dy, dz, c2), (dy, dz, c)
+                goal, event = weight_goal(wave_shift(w), dz)
+                goal, other = goal + c2, record_goal(wave_shift(w), dz) + c2
+            mine, there = (w, dz, c2), (w, dz, c)
             copies += [
                 copy_to(send_w.at[goal], got_w.at[there], sw.at[mine], rw.at[there], space=goal, event=event),
                 copy_to(send_r.at[other], got_r.at[there], sr.at[mine], rr.at[there], space=other),
@@ -289,9 +296,8 @@
         def _():
             receive(w + 1)
 
-        @pl.when(w == 0)
-        def _():
-            start(3)
+        if EARLY == 2:
+            pl.when(w == 0)(lambda: start(3))
 
         @pl.when(w == 3)
         def _():
@@ -507,9 +513,9 @@
 
 
 def step_kernel(
-    send_w, send_r, fwd_now_h, fwd_prev_h, adj_now_h, adj_prev_h, shear_h, density,
+    placed, fwd_now_h, fwd_prev_h, adj_now_h, adj_prev_h, shear_h, density,
     fwd_last, fwd_before, adj_last, adj_before, pieces,
-    fwd_now, fwd_prev, adj_now, adj_prev, shear,
+    fwd_now, fwd_prev, adj_now, adj_prev, shear, send_w, send_r,
     got_w, got_r, left, right, left_part, onehot, total, src,
     zero, one, local, stiff, inv, terms, faces, got_faces, got_density, out_terms, got_terms,
     sw, rw, sr, rr, fs, fr, hs, hr, ds, dr, ts, tr, ins,
@@ -530,6 +536,10 @@
     signal(barrier, space=up)
     signal(barrier, space=down)
 
+    def turn(w):
+        turn_stations(w, placed, send_w, send_r)
+
+    turn(0)
     pl.semaphore_wait(barrier, greeted + 4 + 2)
 
     weigh = [
@@ -554,7 +564,9 @@
     for copy in first_wave:
         copy.start()
     own_stations(send_w, send_r, got_w, got_r, rw, rr)
-    start(1)
+    for w in range(1, EARLY):
+        turn(w)
+        start(w)
 
     for copy in fetch:
         copy.wait()
@@ -616,8 +628,11 @@
     forward = exchange(0, 0, 2)
     arrived(weigh)
     inverse_mass(density[...], got_density, inv)
+    for w in range(EARLY, 4):
+        turn(w)
     receive(0)
-    start(2)
+    if EARLY < 4:
+        start(EARLY)
     gather_sources(got_w, got_r, left, right, left_part, onehot, total, receive, start, shares)
     spread_sources(total, src)
     subtract(0)
@@ -678,7 +693,7 @@
     lax.fori_loop(0, 4, last_shares, 0)
 
 
-def steps(send_w, send_r, fwd_now, fwd_prev, adj_now, adj_prev, shear, density):
+def steps(placed, fwd_now, fwd_prev, adj_now, adj_prev, shear, density):
     fields = pltpu.VMEM((256, 8, 128), F32)
     waves = DMA((4, 4, 2))
     return pl.pallas_call(
@@ -687,11 +702,13 @@
             *[jax.ShapeDtypeStruct((1024, 128), F32)] * 4,
             jax.ShapeDtypeStruct((2, 64, 128), F32),
         ),
-        in_specs=[VM, VM, HBM, HBM, HBM, HBM, HBM, VM],
+        in_specs=[VM, HBM, HBM, HBM, HBM, HBM, VM],
         out_specs=(VM,) * 5,
         scratch_shapes=[
             *[pltpu.VMEM((1024, 128), F32)] * 4,
             pltpu.VMEM((512, 128), F32),
+            pltpu.VMEM((SLABS, DIRECT, CAP), F32),
+            pltpu.VMEM((SLABS, 1, 5 * CAP), F32),
             pltpu.VMEM((4, 4, 2, DIRECT, CAP), F32),
             pltpu.VMEM((4, 4, 2, 1, 5 * CAP), F32),
             pltpu.VMEM((4, 4, 2, 16, CAP), F32),
@@ -720,7 +737,7 @@
         ],
         compiler_params=pltpu.CompilerParams(collective_id=0, has_side_effects=True, vmem_limit_bytes=32 << 20),
         name="steps",
-    )(send_w, send_r, fwd_now, fwd_prev, adj_now, adj_prev, shear, density)
+    )(placed, fwd_now, fwd_prev, adj_now, adj_prev, shear, density)
 
 
 def finish_kernel(a, b, c, d, pieces, shear, a_out, b_out, c_out, d_out, kernel_out, kernel, sems):
@@ -772,11 +789,11 @@
         return pltpu.with_memory_space_constraint(value, pltpu.HBM)
 
     shear = to_rows(shear_mod)
-    send_w, send_r = place(
+    placed = place(
         far(station_owner.T), far(receiver_local.reshape(1, ST)), far(station_weights), far(adj_records)
     )
     found = steps(
-        send_w, send_r, *[far(to_rows(v)) for v in (fwd_now, fwd_prev, adj_now, adj_prev)],
+        placed, *[far(to_rows(v)) for v in (fwd_now, fwd_prev, adj_now, adj_prev)],
         shear, density.reshape(8, 128),
     )
     *fields, kernel = finish(*found, shear)

time: 73.3 us -> 66.7 us (0.910)
  Pallas kernels: 72.5 us -> 65.5 us
    pallas_call x1, Pallas kernels: 62.6 us -> 58.3 us  [steps(): pl.pallas_call(step_kernel, out_shape=(*[jax.ShapeDtypeStruct((1024, 128)...]
    pallas_call x1, Pallas kernels: 8.55 us -> 5.85 us  [place(): pl.pallas_call(place_kernel, out_shape=jax.ShapeDtypeStruct((SLABS * CAP,...]
where the time goes in v3:
time: 66.7 us; the launch traced here: 66.2 us
  Pallas kernels  65.5 us (98%)
  between operations  0.68 us (1%)
    pallas_call x1, Pallas kernels, steps(): pl.pallas_call(step_kernel, out_shape=(*[jax.ShapeDtypeStruct((1024, 128)...  58.3 us
    pallas_call x1, Pallas kernels, place(): pl.pallas_call(place_kernel, out_shape=jax.ShapeDtypeStruct((SLABS * CAP,...  5.85 us
    pallas_call x1, Pallas kernels, finish(): pl.pallas_call(finish_kernel, out_shape=(*[jax.ShapeDtypeStruct((1024, 12...  1.36 us

profile of v3, /device:TPU:2, one launch (start us, length us, event | category | flops | bytes accessed | tf_op | source)
XLA Modules:
  0.0 66.2 jit_solution(13231084007533727162)
XLA Ops:
  0.6 0.0 copy-start.1
  0.6 0.0 copy-start
  0.7 5.8 %place.1.placed = f32[8192,128]{1,0:T(8,128)S(1)} custom-call(s32[1,2048]{1,0:T(1,128)} %bitcast.55, s32[1,2048]{1,0:T(1,128)} %bitcast.56, f32[64,2048]{1,0:T(8,128)} %weights_h.1, f32[2,2,2048]{2,1,0:T(2,128)} %records_h.1), custom_call_target="tpu_custom_call" | custom-call | tf_op jit(solution)/shard_map/place/pallas_call | solution.py:136
  6.5 0.0 copy-done.1
  6.5 0.0 copy-done
  6.5 58.3 %steps.1 = (f32[1024,128]{1,0:T(8,128)S(1)}, f32[1024,128]{1,0:T(8,128)S(1)}, f32[1024,128]{1,0:T(8,128)S(1)}, f32[1024,128]{1,0:T(8,128)S(1)}, f32[2,64,128]{2,1,0:T(8,128)S(1)}) custom-call(f32[8192,128]{1,0:T(8,128)S(1)} %place.1.placed, f32[1024,128]{1,0:T(8,128)} %bitcast.51, f32[1024,128]{1,0:T(8,128)} %bitcast.52, f32[1024,128]{1,0:T(8,128)} %bitcast.53, ...), custom_call_target="tpu_custom_call" | custom-call | tf_op jit(solution)/shard_map/steps/pallas_call | solution.py:699
  64.8 1.4 %finish.1 = (f32[1024,128]{1,0:T(8,128)}, f32[1024,128]{1,0:T(8,128)}, f32[1024,128]{1,0:T(8,128)}, f32[1024,128]{1,0:T(8,128)}, f32[64,128]{1,0:T(8,128)}) custom-call(f32[1024,128]{1,0:T(8,128)S(1)} %get-tuple-element.15.a, f32[1024,128]{1,0:T(8,128)S(1)} %get-tuple-element.16.b, f32[1024,128]{1,0:T(8,128)S(1)} %get-tuple-element.17.c, ...), custom_call_target="tpu_custom_call" | custom-call | tf_op jit(solution)/shard_map/finish/pallas_call | solution.py:765
Async XLA Ops:
  0.6 5.9 %copy-start.1 = (f32[1024]{0:T(1024)S(1)}, f32[1024]{0:T(1024)}, u32[]{:S(2)}) copy-start(f32[1024]{0:T(1024)} %param.15) | copy-start | bytes 12292
  0.6 5.9 %copy-start = (f32[64,1024]{1,0:T(8,128)S(1)}, f32[64,1024]{1,0:T(8,128)}, u32[]{:S(2)}) copy-start(f32[64,1024]{1,0:T(8,128)} %param.14) | copy-start | bytes 786436

commit v4 on v3

--- a/solution.py
+++ b/solution.py
@@ -82,6 +82,12 @@
     ]
     for copy in fetch:
         copy.start()
+
+    def clear(i, carry):
+        placed[pl.ds(pl.multiple_of(i * 128, 128), 128), :] = jnp.zeros((128, 128), F32)
+        return carry
+
+    lax.fori_loop(0, SLABS * CAP // 128, clear, 0)
     fetch[0].wait()
     slab = lax.broadcasted_iota(jnp.int32, (SLABS, 256), 0)
     earlier = (
@@ -115,11 +121,6 @@
         )
         rows[cols, :] = block.T
 
-    def clear(i, carry):
-        placed[pl.ds(pl.multiple_of(i * 128, 128), 128), :] = jnp.zeros((128, 128), F32)
-        return carry
-
-    lax.fori_loop(0, SLABS * CAP // 128, clear, 0)
     copy.wait()
 
     def move(i, carry):

time: 66.7 us -> 66.8 us (level)
  no operation moved by 1% of the time
where the time goes in v4:
time: 66.8 us; the launch traced here: 65.9 us
  Pallas kernels  65.2 us (98%)
  between operations  0.68 us (1%)
    pallas_call x1, Pallas kernels, steps(): pl.pallas_call(step_kernel, out_shape=(*[jax.ShapeDtypeStruct((1024, 128)...  58.3 us
    pallas_call x1, Pallas kernels, place(): pl.pallas_call(place_kernel, out_shape=jax.ShapeDtypeStruct((SLABS * CAP,...  5.58 us
    pallas_call x1, Pallas kernels, finish(): pl.pallas_call(finish_kernel, out_shape=(*[jax.ShapeDtypeStruct((1024, 12...  1.36 us

profile of v4, /device:TPU:2, one launch (start us, length us, event | category | flops | bytes accessed | tf_op | source)
XLA Modules:
  0.0 65.9 jit_solution(18153172393636125481)
XLA Ops:
  0.6 0.0 copy-start.1
  0.6 0.0 copy-start
  0.7 5.6 %place.1.placed = f32[8192,128]{1,0:T(8,128)S(1)} custom-call(s32[1,2048]{1,0:T(1,128)} %bitcast.55, s32[1,2048]{1,0:T(1,128)} %bitcast.56, f32[64,2048]{1,0:T(8,128)} %weights_h.1, f32[2,2,2048]{2,1,0:T(2,128)} %records_h.1), custom_call_target="tpu_custom_call" | custom-call | tf_op jit(solution)/shard_map/place/pallas_call | solution.py:137
  6.2 0.0 copy-done.1
  6.2 0.0 copy-done
  6.3 58.3 %steps.1 = (f32[1024,128]{1,0:T(8,128)S(1)}, f32[1024,128]{1,0:T(8,128)S(1)}, f32[1024,128]{1,0:T(8,128)S(1)}, f32[1024,128]{1,0:T(8,128)S(1)}, f32[2,64,128]{2,1,0:T(8,128)S(1)}) custom-call(f32[8192,128]{1,0:T(8,128)S(1)} %place.1.placed, f32[1024,128]{1,0:T(8,128)} %bitcast.51, f32[1024,128]{1,0:T(8,128)} %bitcast.52, f32[1024,128]{1,0:T(8,128)} %bitcast.53, ...), custom_call_target="tpu_custom_call" | custom-call | tf_op jit(solution)/shard_map/steps/pallas_call | solution.py:700
  64.5 1.4 %finish.1 = (f32[1024,128]{1,0:T(8,128)}, f32[1024,128]{1,0:T(8,128)}, f32[1024,128]{1,0:T(8,128)}, f32[1024,128]{1,0:T(8,128)}, f32[64,128]{1,0:T(8,128)}) custom-call(f32[1024,128]{1,0:T(8,128)S(1)} %get-tuple-element.15.a, f32[1024,128]{1,0:T(8,128)S(1)} %get-tuple-element.16.b, f32[1024,128]{1,0:T(8,128)S(1)} %get-tuple-element.17.c, ...), custom_call_target="tpu_custom_call" | custom-call | tf_op jit(solution)/shard_map/finish/pallas_call | solution.py:766
Async XLA Ops:
  0.6 5.6 %copy-start.1 = (f32[1024]{0:T(1024)S(1)}, f32[1024]{0:T(1024)}, u32[]{:S(2)}) copy-start(f32[1024]{0:T(1024)} %param.15) | copy-start | bytes 12292
  0.6 5.6 %copy-start = (f32[64,1024]{1,0:T(8,128)S(1)}, f32[64,1024]{1,0:T(8,128)}, u32[]{:S(2)}) copy-start(f32[64,1024]{1,0:T(8,128)} %param.14) | copy-start | bytes 786436
